TPU v7x, 256 devices: a whole 4x4x8 slice. The times are simulated.
256 devices in a mesh: gx: 32 (over y, x, core), gz: 8 (over z).
Axes of the slice: x: 4, y: 4, z: 8, core: 2. Of those that a mesh axis runs over, the one named last changes fastest.
Arguments:
- velocity: float32 [64, 3, 128, 64, 256], P(None, None, 'gx', 'gz'), may hold values from -40 to 40
- scaled_modes: float32 [64, 128, 64, 256], P(None, 'gx', 'gz'), may hold values from -70 to 70
Outputs:
- orthonormal: float32 [128, 128, 64, 256], P(None, 'gx', 'gz')
- triangle: float32 [128, 128], replicated
- lower_one: float32 [128, 128], replicated
All inputs are finite; a program needn't handle non-finite values.
Results may differ from a plain program's by a relative error of at most 0.0003.
Values sent between devices are 32-bit elements; how exact they have to be, the bound alone decides.
No kernel may reach another device: no remote copies, remote signals or barrier semaphores. Data moves between devices by JAX's collectives and lax.ppermute only.
A program may use at most 128 MiB of HBM per device.

v0:
```python
import jax
import jax.numpy as jnp
from jax import lax
from jax.experimental import pallas as pl
from jax.experimental.pallas import tpu as pltpu
from jax.sharding import PartitionSpec as P


precise = lax.Precision.HIGHEST
coarse = lax.Precision.DEFAULT
LANES = 128
GRANT = 59 * 2**20
SPANS = ((0, 32), (32, 32))


def pack_faces(velocity, begin, snaps, group=16):
    _, comps, nx, nz, ny = velocity.shape
    skip = begin // group
    halves = ny // LANES
    rows = group * comps * nx

    def kernel(*refs):
        views, (first_x, last_x, first_z, last_z) = refs[:halves], refs[halves:]
        for h, v_ref in enumerate(views):
            lanes = slice(h * LANES, (h + 1) * LANES)
            first_x[:, :, :, lanes] = v_ref[:, :, 0]
            last_x[:, :, :, lanes] = v_ref[:, :, nx - 1]
            flat = v_ref.reshape(rows * nz, LANES)
            first_z[h] = flat[pl.ds(0, rows, stride=nz), :]
            last_z[h] = flat[pl.ds(nz - 1, rows, stride=nz), :]

    face_x = jax.ShapeDtypeStruct((snaps, comps, nz, ny), velocity.dtype)
    face_z = jax.ShapeDtypeStruct((halves, snaps * comps * nx, LANES), velocity.dtype)
    spec_x = pl.BlockSpec((group, comps, nz, ny), lambda i: (i, 0, 0, 0))
    spec_z = pl.BlockSpec((halves, rows, LANES), lambda i: (0, i, 0))
    block = (group, comps, nx, nz, LANES)
    return pl.pallas_call(
        kernel,
        grid=(snaps // group,),
        in_specs=[pl.BlockSpec(block, lambda i, h=h: (i + skip, 0, 0, 0, h)) for h in range(halves)],
        out_specs=[spec_x, spec_x, spec_z, spec_z],
        out_shape=[face_x, face_x, face_z, face_z],
        compiler_params=pltpu.CompilerParams(vmem_limit_bytes=GRANT),
        name="pack_faces",
    )(*[velocity] * halves)


def flatten_modes(modes, group=2):
    count, nx, nz, ny = modes.shape
    halves = ny // LANES

    def kernel(*refs):
        out_ref = refs[halves]
        for h in range(halves):
            flat = refs[h].reshape(count * group * nz, LANES)
            for x in range(group):
                for z in range(nz):
                    start = ((x * halves + h) * nz + z) * LANES
                    out_ref[:, start : start + LANES] = flat[pl.ds(x * nz + z, count, stride=group * nz), :]

    block = (count, group, nz, LANES)
    return pl.pallas_call(
        kernel,
        grid=(nx // group,),
        in_specs=[pl.BlockSpec(block, lambda i, h=h: (0, i, 0, h)) for h in range(halves)],
        out_specs=pl.BlockSpec((count, group * nz * ny), lambda i: (0, i)),
        out_shape=jax.ShapeDtypeStruct((count, nx * nz * ny), modes.dtype),
        compiler_params=pltpu.CompilerParams(vmem_limit_bytes=GRANT),
        name="flatten_modes",
    )(*[modes] * halves)


def criterion(velocity, low_x, high_x, low_z, high_z, begin, group=8):
    _, comps, nx, nz, ny = velocity.shape
    snaps = low_x.shape[0]
    skip = begin // group
    halves = ny // LANES

    def kernel(v_ref, lx_ref, hx_ref, lz_ref, hz_ref, out_ref, q_ref):
        lane = lax.broadcasted_iota(jnp.int32, (nz, LANES), 1)
        level = lax.broadcasted_iota(jnp.int32, (nz, LANES), 0)

        def cut(half):
            return slice(half * LANES, (half + 1) * LANES)

        def wall(parts):
            below = [pltpu.roll(p, 1, 1) for p in parts]
            above = [pltpu.roll(p, LANES - 1, 1) for p in parts]
            out = []
            for h in range(halves):
                here = parts[h]
                fp = jnp.where(lane == LANES - 1, above[h + 1], above[h]) if h < halves - 1 else above[h]
                if h:
                    fm = jnp.where(lane == 0, below[h - 1], below[h])
                else:
                    edge = 3.0 * (here - fp) + pltpu.roll(here, LANES - 2, 1)
                    fm = jnp.where(lane == 0, edge, below[h])
                if h == halves - 1:
                    edge = 3.0 * (here - fm) + pltpu.roll(here, 2, 1)
                    fp = jnp.where(lane == LANES - 1, edge, fp)
                d = fp - fm
                out.append(d)
            return out

        def body(s, carry):
            t = pl.program_id(0) * group + s
            for x in range(nx):
                dx, dz, dy = [], [], []
                for c in range(comps):
                    here = [v_ref[s, c, x, :, cut(h)] for h in range(halves)]
                    dx.append([
                        (v_ref[s, c, x + 1, :, cut(h)] if x < nx - 1 else hx_ref[t, c, :, cut(h)])
                        - (v_ref[s, c, x - 1, :, cut(h)] if x else lx_ref[t, c, :, cut(h)])
                        for h in range(halves)
                    ])
                    row = (t * comps + c) * nx + x
                    part = []
                    for h in range(halves):
                        up = jnp.where(level == nz - 1, hz_ref.at[h][pl.ds(row, nz, stride=0), :], pltpu.roll(here[h], nz - 1, 0))
                        down = jnp.where(level == 0, lz_ref.at[h][pl.ds(row, nz, stride=0), :], pltpu.roll(here[h], 1, 0))
                        part.append(up - down)
                    dz.append(part)
                    dy.append(wall(here))
                for h in range(halves):
                    diagonal = dx[0][h] * dx[0][h] + dz[1][h] * dz[1][h] + dy[2][h] * dy[2][h]
                    cross = dz[0][h] * dx[1][h] + dy[0][h] * dx[2][h] + dy[1][h] * dz[2][h]
                    q_ref[h, pl.ds((s * nx + x) * nz, nz), :] = -0.125 * diagonal - 0.25 * cross
            return carry

        lax.fori_loop(0, group, body, 0, unroll=4)
        for x in range(nx):
            for z in range(nz):
                for h in range(halves):
                    start = ((x * halves + h) * nz + z) * LANES
                    view = q_ref.at[h]
                    out_ref[:, start : start + LANES] = view[pl.ds(x * nz + z, group, stride=nx * nz), :]

    near = pl.BlockSpec(memory_space=pltpu.VMEM)
    return pl.pallas_call(
        kernel,
        grid=(snaps // group,),
        in_specs=[pl.BlockSpec((group, comps, nx, nz, ny), lambda i: (i + skip, 0, 0, 0, 0)), near, near, near, near],
        out_specs=pl.BlockSpec((group, nx * nz * ny), lambda i: (i, 0)),
        out_shape=jax.ShapeDtypeStruct((snaps, nx * nz * ny), velocity.dtype),
        scratch_shapes=[pltpu.VMEM((halves, group * nx * nz, LANES), velocity.dtype)],
        compiler_params=pltpu.CompilerParams(vmem_limit_bytes=GRANT),
        name="criterion",
    )(velocity, *[pltpu.with_memory_space_constraint(halo, pltpu.VMEM) for halo in (low_x, high_x, low_z, high_z)])


def spread(row, shape):
    return jnp.broadcast_to(row, shape)


def three_parts(value):
    first = value.astype(jnp.bfloat16).astype(jnp.float32)
    rest = value - first
    second = rest.astype(jnp.bfloat16).astype(jnp.float32)
    return first, second, rest - second


def eliminate(a_ref, x_ref, u_ref):
    size = a_ref.shape[0]
    tall = 8
    row = lax.broadcasted_iota(jnp.int32, (tall, size), 0)
    lane = lax.broadcasted_iota(jnp.int32, (tall, size), 1)
    full = (tall, size)
    full_row = lax.broadcasted_iota(jnp.int32, (size, size), 0)
    full_lane = lax.broadcasted_iota(jnp.int32, (size, size), 1)
    x_ref[...] = jnp.where(full_row == full_lane, 1.0, 0.0)
    for start in range(0, size, tall):
        rows = slice(start, start + tall)
        left, right = a_ref[rows, :], x_ref[rows, :]
        columns = [spread(left[:, start + j : start + j + 1], full) for j in range(tall)]
        pivots = jnp.ones(full, jnp.float32)
        for j in range(tall):
            pivot = spread(columns[j][j : j + 1, :], full)
            pivots = jnp.where(row == j, pivot, pivots)
            if j == tall - 1:
                break
            factor = jnp.where(row > j, columns[j] * (1.0 / pivot), 0.0)
            for k in range(j + 1, tall):
                columns[k] = columns[k] - factor * spread(columns[k][j : j + 1, :], full)
            left = left - factor * spread(left[j : j + 1, :], full)
            right = right - factor * spread(right[j : j + 1, :], full)
        scale = 1.0 / jnp.sqrt(pivots)
        left = jnp.where(lane >= start + row, left * scale, 0.0)
        right = right * scale
        u_ref[rows, :] = left
        x_ref[rows, :] = right
        if start + tall < size:
            l1, l2, l3 = three_parts(left)
            r1, r2, r3 = three_parts(right)
            lhs = jnp.concatenate([l1, l1, l2, l2, l1, l3], 0).astype(jnp.bfloat16)
            rhs_left = jnp.concatenate([l1, l2, l1, l2, l3, l1], 0).astype(jnp.bfloat16)
            rhs_right = jnp.concatenate([r1, r2, r1, r2, r3, r1], 0).astype(jnp.bfloat16)
            rhs = jnp.concatenate([rhs_left, rhs_right], 1)
            change = lax.dot_general(lhs, rhs, (((0,), (0,)), ((), ())), preferred_element_type=jnp.float32)
            below = slice(start + tall, size)
            a_ref[below, :] -= change[start + tall :, :size]
            x_ref[below, :] -= change[start + tall :, size:]


def matmul(left, right, dims=((1,), (0,)), precision=precise):
    return lax.dot_general(left, right, (dims, ((), ())), precision=precision, preferred_element_type=jnp.float32)


def split(value, top):
    big = top * (1.5 * 2.0**16)
    first = (value + big) - big
    rest = value - first
    second = rest.astype(jnp.bfloat16).astype(jnp.float32)
    rest = rest - second
    third = rest.astype(jnp.bfloat16).astype(jnp.float32)
    return first, second, third, rest - third


def residual(gram, upper):
    parts = [p.astype(jnp.bfloat16) for p in split(upper, jnp.max(jnp.abs(upper), 0, keepdims=True))]

    def cross(i, j):
        return lax.dot_general(parts[i], parts[j], (((0,), (0,)), ((), ())), preferred_element_type=jnp.float32)

    out = gram - cross(0, 0)
    both = cross(1, 0)
    out = out - (both + both.T)
    both = cross(2, 0) + (cross(3, 0) + cross(2, 1))
    return out - (cross(1, 1) + (both + both.T))


def factor(mine, other, core, cells):
    size = mine.shape[2]
    half = size // 2
    quarter = half // 2

    def kernel(core_ref, mine_ref, other_ref, weight_ref, triangle_ref, lower_ref, a_ref, x_ref, u_ref, y_ref, v_ref):
        full_row = lax.broadcasted_iota(jnp.int32, (size, size), 0)
        full_lane = lax.broadcasted_iota(jnp.int32, (size, size), 1)
        first = core_ref[0] == 0

        def whole(k):
            low = jnp.where(first, mine_ref[k], other_ref[k])
            high = jnp.where(first, other_ref[k], mine_ref[k])
            base = jnp.concatenate([low[:quarter], high[:quarter]], 0) * (1.0 / cells)
            diagonal = jnp.broadcast_to(low[quarter : quarter + 1] * (1.0 / cells), (size, size))
            rows = jnp.concatenate([base, pltpu.roll(base, half, 1)], 0)
            late = full_row >= half
            inside = jnp.logical_and(full_lane >= half, full_lane < full_row)
            own = jnp.logical_or(
                jnp.logical_and(jnp.logical_not(late), full_lane >= full_row), jnp.logical_and(late, inside)
            )
            rows = jnp.where(own, rows, rows.T)
            return jnp.where(jnp.logical_and(late, full_lane == full_row), diagonal, rows)

        gram, extra = whole(0), whole(1)
        a_ref[...] = gram
        eliminate(a_ref, x_ref, u_ref)
        upper = u_ref[...]
        eye = jnp.where(full_row == full_lane, 1.0, 0.0)
        inverse = refined(x_ref[...], upper, eye)
        lower_ref[...] = upper.T
        rest = residual(gram, upper) + extra
        change = matmul(matmul(inverse, rest), inverse, ((1,), (1,)))
        change = jnp.where(full_lane <= full_row, change, change.T)
        small = jnp.sum(change * change) < 2.0**-12

        @pl.when(small)
        def _():
            keep = jnp.where(full_lane < full_row, 1.0, jnp.where(full_lane == full_row, 0.5, 0.0))
            step = keep * change
            for precision in (coarse, coarse, precise):
                step = keep * (change - matmul(step, step, ((1,), (1,)), precision))
            weight = inverse
            for precision in (coarse, coarse, precise, precise):
                weight = inverse - matmul(step, weight, precision=precision)
            weight_ref[...] = weight
            triangle_ref[...] = upper + matmul(step, upper, ((0,), (0,)))

        @pl.when(jnp.logical_not(small))
        def _():
            a_ref[...] = change + eye
            eliminate(a_ref, y_ref, v_ref)
            weight_ref[...] = matmul(refined(y_ref[...], v_ref[...], eye), inverse)
            triangle_ref[...] = matmul(v_ref[...], upper)

    square = jax.ShapeDtypeStruct((size, size), jnp.float32)
    vmem = pl.BlockSpec(memory_space=pltpu.VMEM)
    return pl.pallas_call(
        kernel,
        in_specs=[pl.BlockSpec(memory_space=pltpu.SMEM), vmem, vmem],
        out_specs=[vmem, vmem, vmem],
        out_shape=[square, square, square],
        scratch_shapes=[pltpu.VMEM((size, size), jnp.float32)] * 5,
        name="factor",
    )(core, *[pltpu.with_memory_space_constraint(value, pltpu.VMEM) for value in (mine, other)])


def refined(inverse, upper, eye):
    return inverse + matmul(eye - matmul(inverse, upper, ((1,), (1,))), inverse)


def two_sum(left, right):
    total = left + right
    back = total - left
    return total, (left - (total - back)) + (right - back)


def gram_halves(parts, core, chunk=2048, piece=512):
    cells = parts[0].shape[1]
    count = len(parts)
    size = sum(part.shape[0] for part in parts)
    half, quarter = size // 2, size // 4
    steps = cells // chunk

    def kernel(core_ref, *refs):
        part_refs = refs[:count]
        keep_ref, send_ref, high_ref, low_ref, cross_ref = refs[count:]
        step = pl.program_id(0)

        @pl.when(step == 0)
        def _():
            high_ref[...] = jnp.zeros_like(high_ref)
            low_ref[...] = jnp.zeros_like(low_ref)
            cross_ref[...] = jnp.zeros_like(cross_ref)

        for k in range(chunk // piece):
            span = slice(k * piece, (k + 1) * piece)
            block = jnp.concatenate([ref[:, span] for ref in part_refs], 0)
            first, second, third, _ = split(block, jnp.max(jnp.abs(block), 1, keepdims=True))
            lhs = jnp.concatenate([first, second, third], 0).astype(jnp.bfloat16)
            part = lax.dot_general(
                lhs, lhs[: 2 * size], (((1,), (1,)), ((), ())), preferred_element_type=jnp.float32
            )
            high_ref[...], error = two_sum(high_ref[...], part[:size, :size])
            low_ref[...] += error + part[size : 2 * size, size:]
            cross_ref[...] += part[size : 2 * size, :size] + (part[2 * size :, :size] + part[2 * size :, size:])

        @pl.when(step == steps - 1)
        def _():
            cross = cross_ref[...]
            high_ref[...], low_ref[...] = two_sum(high_ref[...], low_ref[...] + (cross + cross.T))
            lane = lax.broadcasted_iota(jnp.int32, (half, size), 1)
            row = lax.broadcasted_iota(jnp.int32, (half, size), 0)
            lead = core_ref[0] == 0
            for k, ref in enumerate((high_ref, low_ref)):
                corner = ref[half:, :]
                base = jnp.where(lane < row, pltpu.roll(corner, half, 1), ref[:half, :])
                diagonal = jnp.sum(jnp.where(lane == row + half, corner, 0.0), 0, keepdims=True)
                extra = jnp.broadcast_to(diagonal, (8, size))
                low = jnp.concatenate([base[:quarter], extra], 0)
                high = jnp.concatenate([base[quarter:], extra], 0)
                keep_ref[k] = jnp.where(lead, low, high)
                send_ref[k] = jnp.where(lead, high, low)

    out = jax.ShapeDtypeStruct((2, quarter + 8, size), jnp.float32)
    spec = pl.BlockSpec((2, quarter + 8, size), lambda i: (0, 0, 0))
    return pl.pallas_call(
        kernel,
        grid=(steps,),
        in_specs=[
            pl.BlockSpec(memory_space=pltpu.SMEM),
            *[pl.BlockSpec((part.shape[0], chunk), lambda i: (0, i)) for part in parts],
        ],
        out_specs=[spec, spec],
        out_shape=[out, out],
        scratch_shapes=[pltpu.VMEM((size, size), jnp.float32)] * 3,
        name="gram_halves",
    )(core, *parts)


def apply_split(weight, parts, nx, nz, ny):
    count = sum(part.shape[0] for part in parts)
    halves = ny // LANES

    def kernel(w_ref, *refs):
        part_refs, out_ref = refs[:-1], refs[-1]
        w1, w2, w3 = three_parts(w_ref[...])
        lhs = jnp.concatenate(
            [
                jnp.concatenate([w1, w2], 1),
                jnp.concatenate([w2, w1], 1),
                jnp.concatenate([w3, jnp.zeros_like(w3)], 1),
            ],
            0,
        ).astype(jnp.bfloat16)
        block = jnp.concatenate([ref[...] for ref in part_refs], 0)
        s1, s2, s3 = three_parts(block)
        pair = jnp.concatenate([s1, s2], 0).astype(jnp.bfloat16)
        dims = (((1,), (0,)), ((), ()))
        main = lax.dot_general(lhs, pair, dims, preferred_element_type=jnp.float32)
        tail = lax.dot_general(w1.astype(jnp.bfloat16), s3.astype(jnp.bfloat16), dims, preferred_element_type=jnp.float32)
        result = main[:count] + (main[count : 2 * count] + (main[2 * count :] + tail))
        flat = out_ref.reshape(count * nz, LANES)
        for z in range(nz):
            flat[pl.ds(z, count, stride=nz), :] = result[:, z * LANES : (z + 1) * LANES]

    return pl.pallas_call(
        kernel,
        grid=(nx, halves),
        in_specs=[
            pl.BlockSpec((count, count), lambda i, h: (0, 0)),
            *[pl.BlockSpec((part.shape[0], nz * LANES), lambda i, h: (0, i * halves + h)) for part in parts],
        ],
        out_specs=pl.BlockSpec((count, 1, nz, LANES), lambda i, h: (0, i, 0, h)),
        out_shape=jax.ShapeDtypeStruct((count, nx, nz, ny), jnp.float32),
        name="apply_split",
    )(weight, *parts)


def shifted(value, axis, forward):
    count = lax.axis_size(axis)
    step = 1 if forward else count - 1
    return lax.ppermute(value, axis, [(i, (i + step) % count) for i in range(count)])


def flipped(value, flip_x, flip_z):
    size_x, size_z = lax.axis_size("gx"), lax.axis_size("gz")
    pairs = [
        (x * size_z + z, (x ^ flip_x) * size_z + (z ^ flip_z)) for x in range(size_x) for z in range(size_z)
    ]
    return lax.ppermute(value, ("gx", "gz"), pairs)


def pair_sum(left, right):
    high, error = two_sum(left[0], right[0])
    return jnp.stack([high, left[1] + right[1] + error])


def all_sum(keep, send):
    value = pair_sum(keep, flipped(send, 1, 0))
    flips = [(2, 0), (6, 0), (8, 0), (24, 0), (0, 1), (0, 2), (0, 6)]
    for flip_x, flip_z in flips:
        value = pair_sum(value, flipped(value, flip_x, flip_z))
    return value, flipped(value, 1, 0)


def shards(velocity, scaled_modes):
    _, _, cells_x, cells_z, cells_y = velocity.shape
    total_cells = cells_x * lax.axis_size("gx") * cells_z * lax.axis_size("gz") * cells_y
    core = (lax.axis_index("gx") % 2).astype(jnp.int32).reshape(1)
    halos = []
    for begin, count in SPANS:
        first_x, last_x, first_z, last_z = pack_faces(velocity, begin, count)
        low_x = shifted(last_x, "gx", True)
        high_x = shifted(first_x, "gx", False)
        low_z = shifted(last_z, "gz", True)
        high_z = shifted(first_z, "gz", False)
        halos.append((low_x, high_x, low_z, high_z))
    parts = [flatten_modes(scaled_modes)]
    for (begin, _), halo in zip(SPANS, halos):
        parts.append(criterion(velocity, *halo, begin))
    mine, other = all_sum(*gram_halves(parts, core))
    weight, triangle, lower_one = factor(mine, other, core, float(total_cells))
    basis = apply_split(weight, parts, cells_x, cells_z, cells_y)
    return basis, triangle, lower_one


def solution(mesh):
    in_specs = (P(None, None, "gx", "gz", None), P(None, "gx", "gz", None))
    out_specs = (P(None, "gx", "gz", None), P(), P())
    return jax.shard_map(shards, mesh=mesh, in_specs=in_specs, out_specs=out_specs, check_vma=False)
```

profile of v0, /device:TPU:1, one launch (start us, length us, event | category | flops | bytes accessed | tf_op | source)
XLA Modules:
  0.0 105.4 jit_solution(5601902299194752958)
XLA Ops:
  0.6 3.0 %pack_faces.2 = (f32[32,3,8,256]{3,2,1,0:T(8,128)}, f32[32,3,8,256]{3,2,1,0:T(8,128)}, f32[2,384,128]{2,1,0:T(8,128)}, f32[2,384,128]{2,1,0:T(8,128)}) custom-call(f32[64,3,4,8,256]{4,3,2,1,0:T(8,128)} %v_ref.3, f32[64,3,4,8,256]{4,3,2,1,0:T(8,128)} %v_ref.3), custom_call_target="tpu_custom_call" | custom-call | tf_op jit(solution)/shard_map/pack_faces/pallas_call | solution.py:37
  3.6 2.6 %collective-permute-start = (f32[32,3,8,256]{3,2,1,0:T(8,128)}, f32[32,3,8,256]{3,2,1,0:T(8,128)S(1)}, u32[]{:S(2)}, u32[]{:S(2)}) collective-permute-start(f32[32,3,8,256]{3,2,1,0:T(8,128)} %get-tuple-element.16), channel_id=1, source_target_pairs={{0,8},{8,16},{16,24},{24,32},{32,40},{40,48},{48,56},{56,64},{64,7... | collective-permute-start | bytes 2359304 | tf_op jit(solution)/shard_map/ppermute | solution.py:413
  6.2 1.6 %collective-permute-start.2 = (f32[2,384,128]{2,1,0:T(8,128)}, f32[2,384,128]{2,1,0:T(8,128)S(1)}, u32[]{:S(2)}, u32[]{:S(2)}) collective-permute-start(f32[2,384,128]{2,1,0:T(8,128)} %get-tuple-element.18), channel_id=1, source_target_pairs={{0,1},{1,2},{2,3},{3,4},{4,5},{5,6},{6,7},{7,0},{8,9},{9,10},{10,1... | collective-permute-start | bytes 1179656 | tf_op jit(solution)/shard_map/ppermute | solution.py:413
  7.9 3.9 %collective-permute-start.3 = (f32[2,384,128]{2,1,0:T(8,128)}, f32[2,384,128]{2,1,0:T(8,128)S(1)}, u32[]{:S(2)}, u32[]{:S(2)}) collective-permute-start(f32[2,384,128]{2,1,0:T(8,128)} %get-tuple-element.19), channel_id=1, source_target_pairs={{0,7},{1,0},{2,1},{3,2},{4,3},{5,4},{6,5},{7,6},{8,15},{9,8},{10,9... | collective-permute-start | bytes 1179656 | tf_op jit(solution)/shard_map/ppermute | solution.py:413
  11.8 3.1 %pack_faces.3 = (f32[32,3,8,256]{3,2,1,0:T(8,128)}, f32[32,3,8,256]{3,2,1,0:T(8,128)}, f32[2,384,128]{2,1,0:T(8,128)}, f32[2,384,128]{2,1,0:T(8,128)}) custom-call(f32[64,3,4,8,256]{4,3,2,1,0:T(8,128)} %v_ref.3, f32[64,3,4,8,256]{4,3,2,1,0:T(8,128)} %v_ref.3), custom_call_target="tpu_custom_call" | custom-call | tf_op jit(solution)/shard_map/pack_faces/pallas_call | solution.py:37
  14.9 1.7 %collective-permute-start.4 = (f32[32,3,8,256]{3,2,1,0:T(8,128)}, f32[32,3,8,256]{3,2,1,0:T(8,128)S(1)}, u32[]{:S(2)}, u32[]{:S(2)}) collective-permute-start(f32[32,3,8,256]{3,2,1,0:T(8,128)} %get-tuple-element.20), channel_id=1, source_target_pairs={{0,8},{8,16},{16,24},{24,32},{32,40},{40,48},{48,56},{56,64},{64,7... | collective-permute-start | bytes 2359304 | tf_op jit(solution)/shard_map/ppermute | solution.py:413
  16.6 4.2 %collective-permute-done.2.lz_ref = f32[2,384,128]{2,1,0:T(8,128)S(1)} collective-permute-done((f32[2,384,128]{2,1,0:T(8,128)}, f32[2,384,128]{2,1,0:T(8,128)S(1)}, u32[]{:S(2)}, u32[]{:S(2)}) %collective-permute-start.2) | collective-permute-done | bytes 393248 | tf_op jit(solution)/shard_map/ppermute | solution.py:413
  20.9 0.7 copy-done
  21.6 3.1 %collective-permute-start.7 = (f32[2,384,128]{2,1,0:T(8,128)}, f32[2,384,128]{2,1,0:T(8,128)}, u32[]{:S(2)}, u32[]{:S(2)}) collective-permute-start(f32[2,384,128]{2,1,0:T(8,128)} %get-tuple-element.23), channel_id=1, source_target_pairs={{0,7},{1,0},{2,1},{3,2},{4,3},{5,4},{6,5},{7,6},{8,15},{9,8},{10,9... | collective-permute-start | bytes 1179656 | tf_op jit(solution)/shard_map/ppermute | solution.py:413
  24.7 3.0 %flatten_modes.1.refs_0_ = f32[64,8192]{1,0:T(8,128)} custom-call(f32[64,4,8,256]{3,2,1,0:T(8,128)} %refs_1_.3, f32[64,4,8,256]{3,2,1,0:T(8,128)} %refs_1_.3), custom_call_target="tpu_custom_call" | custom-call | tf_op jit(solution)/shard_map/flatten_modes/pallas_call | solution.py:62
  27.7 6.2 %criterion.2.refs_1_ = f32[32,8192]{1,0:T(8,128)} custom-call(f32[64,3,4,8,256]{4,3,2,1,0:T(8,128)} %v_ref.3, f32[32,3,8,256]{3,2,1,0:T(8,128)S(1)} %collective-permute-done.lx_ref, f32[32,3,8,256]{3,2,1,0:T(8,128)} %collective-permute-done.1.hx_ref, f32[2,384,128]{2,1,0:T(8,128)S(1)} %collective-permute-done.2.lz_ref, f32[2,384,128]{2,1,0:T(8,128)S(1)} %copy-done.1), custom_call_target="tpu_custom_call" | custom-call | tf_op jit(solution)/shard_map/criterion/pallas_call | solution.py:139
  34.0 6.2 %criterion.3.refs_2_ = f32[32,8192]{1,0:T(8,128)} custom-call(f32[64,3,4,8,256]{4,3,2,1,0:T(8,128)} %v_ref.3, f32[32,3,8,256]{3,2,1,0:T(8,128)S(1)} %collective-permute-done.4.lx_ref, f32[32,3,8,256]{3,2,1,0:T(8,128)S(1)} %collective-permute-done.5.hx_ref, f32[2,384,128]{2,1,0:T(8,128)} %collective-permute-done.6.lz_ref, ...), custom_call_target="tpu_custom_call" | custom-call | tf_op jit(solution)/shard_map/criterion/pallas_call | solution.py:139
  40.2 5.6 %gram_halves.1 = (f32[2,40,128]{2,1,0:T(8,128)}, f32[2,40,128]{2,1,0:T(8,128)}) custom-call(s32[1]{0:T(128)} %bitcast.core_ref, f32[64,8192]{1,0:T(8,128)} %flatten_modes.1.refs_0_, f32[32,8192]{1,0:T(8,128)} %criterion.2.refs_1_, f32[32,8192]{1,0:T(8,128)} %criterion.3.refs_2_), custom_call_target="tpu_custom_call" | custom-call | tf_op jit(solution)/shard_map/gram_halves/pallas_call | solution.py:357
  45.8 4.4 %collective-permute-start.8 = (f32[2,40,128]{2,1,0:T(8,128)}, f32[2,40,128]{2,1,0:T(8,128)S(1)}, u32[]{:S(2)}, u32[]{:S(2)}) collective-permute-start(f32[2,40,128]{2,1,0:T(8,128)} %get-tuple-element.25), channel_id=1, source_target_pairs={{0,8},{1,9},{2,10},{3,11},{4,12},{5,13},{6,14},{7,15},{8,0},{9,1},... | collective-permute-start | bytes 122888 | tf_op jit(solution)/shard_map/ppermute | solution.py:421
  50.2 1.1 %collective-permute-done.8 = f32[2,40,128]{2,1,0:T(8,128)S(1)} collective-permute-done((f32[2,40,128]{2,1,0:T(8,128)}, f32[2,40,128]{2,1,0:T(8,128)S(1)}, u32[]{:S(2)}, u32[]{:S(2)}) %collective-permute-start.8) | collective-permute-done | bytes 40992 | tf_op jit(solution)/shard_map/ppermute | solution.py:421
  51.3 0.8 fusion.7
  52.1 2.8 %collective-permute-done.9 = f32[2,40,128]{2,1,0:T(8,128)S(1)} collective-permute-done((f32[2,40,128]{2,1,0:T(8,128)S(1)}, f32[2,40,128]{2,1,0:T(8,128)S(1)}, u32[]{:S(2)}, u32[]{:S(2)}) %collective-permute-start.9) | collective-permute-done | bytes 40992 | tf_op jit(solution)/shard_map/ppermute | solution.py:421
  55.1 4.0 %collective-permute-done.10 = f32[2,40,128]{2,1,0:T(8,128)S(1)} collective-permute-done((f32[2,40,128]{2,1,0:T(8,128)S(1)}, f32[2,40,128]{2,1,0:T(8,128)S(1)}, u32[]{:S(2)}, u32[]{:S(2)}) %collective-permute-start.10) | collective-permute-done | bytes 40992 | tf_op jit(solution)/shard_map/ppermute | solution.py:421
  59.2 0.1 collective-permute-start.11
  59.3 2.8 %collective-permute-done.11 = f32[2,40,128]{2,1,0:T(8,128)S(1)} collective-permute-done((f32[2,40,128]{2,1,0:T(8,128)S(1)}, f32[2,40,128]{2,1,0:T(8,128)S(1)}, u32[]{:S(2)}, u32[]{:S(2)}) %collective-permute-start.11) | collective-permute-done | bytes 40992 | tf_op jit(solution)/shard_map/ppermute | solution.py:421
  62.2 1.3 %collective-permute-start.12 = (f32[2,40,128]{2,1,0:T(8,128)S(1)}, f32[2,40,128]{2,1,0:T(8,128)S(1)}, u32[]{:S(2)}, u32[]{:S(2)}) collective-permute-start(f32[2,40,128]{2,1,0:T(8,128)S(1)} %pad_maximum_fusion.3), channel_id=1, source_target_pairs={{0,192},{1,193},{2,194},{3,195},{4,196},{5,197},{6,198},{7,199},{8... | collective-permute-start | bytes 122888 | tf_op jit(solution)/shard_map/ppermute | solution.py:421
  63.5 2.9 %collective-permute-done.12 = f32[2,40,128]{2,1,0:T(8,128)S(1)} collective-permute-done((f32[2,40,128]{2,1,0:T(8,128)S(1)}, f32[2,40,128]{2,1,0:T(8,128)S(1)}, u32[]{:S(2)}, u32[]{:S(2)}) %collective-permute-start.12) | collective-permute-done | bytes 40992 | tf_op jit(solution)/shard_map/ppermute | solution.py:421
  66.3 0.3 collective-permute-start.13
  66.6 2.8 %collective-permute-done.13 = f32[2,40,128]{2,1,0:T(8,128)S(1)} collective-permute-done((f32[2,40,128]{2,1,0:T(8,128)S(1)}, f32[2,40,128]{2,1,0:T(8,128)S(1)}, u32[]{:S(2)}, u32[]{:S(2)}) %collective-permute-start.13) | collective-permute-done | bytes 40992 | tf_op jit(solution)/shard_map/ppermute | solution.py:421
  69.5 0.4 collective-permute-start.14
  69.8 3.9 %collective-permute-done.14 = f32[2,40,128]{2,1,0:T(8,128)S(1)} collective-permute-done((f32[2,40,128]{2,1,0:T(8,128)S(1)}, f32[2,40,128]{2,1,0:T(8,128)S(1)}, u32[]{:S(2)}, u32[]{:S(2)}) %collective-permute-start.14) | collective-permute-done | bytes 40992 | tf_op jit(solution)/shard_map/ppermute | solution.py:421
  73.7 1.4 %collective-permute-start.15 = (f32[2,40,128]{2,1,0:T(8,128)S(1)}, f32[2,40,128]{2,1,0:T(8,128)S(1)}, u32[]{:S(2)}, u32[]{:S(2)}) collective-permute-start(f32[2,40,128]{2,1,0:T(8,128)S(1)} %pad_maximum_fusion.6), channel_id=1, source_target_pairs={{0,6},{1,7},{2,4},{3,5},{4,2},{5,3},{6,0},{7,1},{8,14},{9,15},{10,... | collective-permute-start | bytes 122888 | tf_op jit(solution)/shard_map/ppermute | solution.py:421
  75.1 3.7 %collective-permute-done.15 = f32[2,40,128]{2,1,0:T(8,128)S(1)} collective-permute-done((f32[2,40,128]{2,1,0:T(8,128)S(1)}, f32[2,40,128]{2,1,0:T(8,128)S(1)}, u32[]{:S(2)}, u32[]{:S(2)}) %collective-permute-start.15) | collective-permute-done | bytes 40992 | tf_op jit(solution)/shard_map/ppermute | solution.py:421
  78.8 8.1 %collective-permute-start.16 = (f32[2,40,128]{2,1,0:T(8,128)S(1)}, f32[2,40,128]{2,1,0:T(8,128)S(1)}, u32[]{:S(2)}, u32[]{:S(2)}) collective-permute-start(f32[2,40,128]{2,1,0:T(8,128)S(1)} %pad_maximum_fusion.7.mine_ref), channel_id=1, source_target_pairs={{0,8},{1,9},{2,10},{3,11},{4,12},{5,13},{6,14},{7,15},{8,0},{9,1},... | collective-permute-start | bytes 122888 | tf_op jit(solution)/shard_map/ppermute | solution.py:421
  86.9 0.9 collective-permute-done.16.other_ref
  87.8 9.4 %factor.1 = (f32[128,128]{1,0:T(8,128)}, f32[128,128]{1,0:T(8,128)}, f32[128,128]{1,0:T(8,128)}) custom-call(s32[1]{0:T(128)} %bitcast.core_ref, f32[2,40,128]{2,1,0:T(8,128)S(1)} %pad_maximum_fusion.7.mine_ref, f32[2,40,128]{2,1,0:T(8,128)S(1)} %collective-permute-done.16.other_ref), custom_call_target="tpu_custom_call" | custom-call | tf_op jit(solution)/shard_map/factor/pallas_call | solution.py:288
  97.2 8.2 %apply_split.1 = f32[128,4,8,256]{3,2,1,0:T(8,128)} custom-call(f32[128,128]{1,0:T(8,128)} %get-tuple-element.26.w_ref, f32[64,8192]{1,0:T(8,128)} %flatten_modes.1.refs_0_, f32[32,8192]{1,0:T(8,128)} %criterion.2.refs_1_, f32[32,8192]{1,0:T(8,128)} %criterion.3.refs_2_), custom_call_target="tpu_custom_call" | custom-call | tf_op jit(solution)/shard_map/apply_split/pallas_call | solution.py:397
  (30 shorter events, 0.4 us)
Async XLA Ops:
  3.6 18.0 %collective-permute-start = (f32[32,3,8,256]{3,2,1,0:T(8,128)}, f32[32,3,8,256]{3,2,1,0:T(8,128)S(1)}, u32[]{:S(2)}, u32[]{:S(2)}) collective-permute-start(f32[32,3,8,256]{3,2,1,0:T(8,128)} %get-tuple-element.16), channel_id=1, source_target_pairs={{0,8},{8,16},{16,24},{24,32},{32,40},{40,48},{48,56},{56,64},{64,7... | collective-permute-start | bytes 2359304 | tf_op jit(solution)/shard_map/ppermute | solution.py:413
  6.2 14.6 %collective-permute-start.2 = (f32[2,384,128]{2,1,0:T(8,128)}, f32[2,384,128]{2,1,0:T(8,128)S(1)}, u32[]{:S(2)}, u32[]{:S(2)}) collective-permute-start(f32[2,384,128]{2,1,0:T(8,128)} %get-tuple-element.18), channel_id=1, source_target_pairs={{0,1},{1,2},{2,3},{3,4},{4,5},{5,6},{6,7},{7,0},{8,9},{9,10},{10,1... | collective-permute-start | bytes 1179656 | tf_op jit(solution)/shard_map/ppermute | solution.py:413
  7.9 13.0 %collective-permute-start.3 = (f32[2,384,128]{2,1,0:T(8,128)}, f32[2,384,128]{2,1,0:T(8,128)S(1)}, u32[]{:S(2)}, u32[]{:S(2)}) collective-permute-start(f32[2,384,128]{2,1,0:T(8,128)} %get-tuple-element.19), channel_id=1, source_target_pairs={{0,7},{1,0},{2,1},{3,2},{4,3},{5,4},{6,5},{7,6},{8,15},{9,8},{10,9... | collective-permute-start | bytes 1179656 | tf_op jit(solution)/shard_map/ppermute | solution.py:413
  11.8 15.9 %collective-permute-start.1 = (f32[32,3,8,256]{3,2,1,0:T(8,128)}, f32[32,3,8,256]{3,2,1,0:T(8,128)}, u32[]{:S(2)}, u32[]{:S(2)}) collective-permute-start(f32[32,3,8,256]{3,2,1,0:T(8,128)} %get-tuple-element.17), channel_id=1, source_target_pairs={{0,248},{8,0},{16,8},{24,16},{32,24},{40,32},{48,40},{56,48},{64,5... | collective-permute-start | bytes 2359304 | tf_op jit(solution)/shard_map/ppermute | solution.py:413
  14.9 19.1 %collective-permute-start.4 = (f32[32,3,8,256]{3,2,1,0:T(8,128)}, f32[32,3,8,256]{3,2,1,0:T(8,128)S(1)}, u32[]{:S(2)}, u32[]{:S(2)}) collective-permute-start(f32[32,3,8,256]{3,2,1,0:T(8,128)} %get-tuple-element.20), channel_id=1, source_target_pairs={{0,8},{8,16},{16,24},{24,32},{32,40},{40,48},{48,56},{56,64},{64,7... | collective-permute-start | bytes 2359304 | tf_op jit(solution)/shard_map/ppermute | solution.py:413
  20.9 13.1 %collective-permute-start.5 = (f32[32,3,8,256]{3,2,1,0:T(8,128)}, f32[32,3,8,256]{3,2,1,0:T(8,128)S(1)}, u32[]{:S(2)}, u32[]{:S(2)}) collective-permute-start(f32[32,3,8,256]{3,2,1,0:T(8,128)} %get-tuple-element.21), channel_id=1, source_target_pairs={{0,248},{8,0},{16,8},{24,16},{32,24},{40,32},{48,40},{56,48},{64,5... | collective-permute-start | bytes 2359304 | tf_op jit(solution)/shard_map/ppermute | solution.py:413
  20.9 0.7 copy-start
  21.6 6.1 %copy-start.1 = (f32[2,384,128]{2,1,0:T(8,128)S(1)}, f32[2,384,128]{2,1,0:T(8,128)}, u32[]{:S(2)}) copy-start(f32[2,384,128]{2,1,0:T(8,128)} %copy-done) | copy-start | bytes 1179652
  21.6 12.3 %collective-permute-start.6 = (f32[2,384,128]{2,1,0:T(8,128)}, f32[2,384,128]{2,1,0:T(8,128)}, u32[]{:S(2)}, u32[]{:S(2)}) collective-permute-start(f32[2,384,128]{2,1,0:T(8,128)} %get-tuple-element.22), channel_id=1, source_target_pairs={{0,1},{1,2},{2,3},{3,4},{4,5},{5,6},{6,7},{7,0},{8,9},{9,10},{10,1... | collective-permute-start | bytes 1179656 | tf_op jit(solution)/shard_map/ppermute | solution.py:413
  21.6 12.3 %collective-permute-start.7 = (f32[2,384,128]{2,1,0:T(8,128)}, f32[2,384,128]{2,1,0:T(8,128)}, u32[]{:S(2)}, u32[]{:S(2)}) collective-permute-start(f32[2,384,128]{2,1,0:T(8,128)} %get-tuple-element.23), channel_id=1, source_target_pairs={{0,7},{1,0},{2,1},{3,2},{4,3},{5,4},{6,5},{7,6},{8,15},{9,8},{10,9... | collective-permute-start | bytes 1179656 | tf_op jit(solution)/shard_map/ppermute | solution.py:413
  45.8 5.5 %collective-permute-start.8 = (f32[2,40,128]{2,1,0:T(8,128)}, f32[2,40,128]{2,1,0:T(8,128)S(1)}, u32[]{:S(2)}, u32[]{:S(2)}) collective-permute-start(f32[2,40,128]{2,1,0:T(8,128)} %get-tuple-element.25), channel_id=1, source_target_pairs={{0,8},{1,9},{2,10},{3,11},{4,12},{5,13},{6,14},{7,15},{8,0},{9,1},... | collective-permute-start | bytes 122888 | tf_op jit(solution)/shard_map/ppermute | solution.py:421
  52.0 2.9 %collective-permute-start.9 = (f32[2,40,128]{2,1,0:T(8,128)S(1)}, f32[2,40,128]{2,1,0:T(8,128)S(1)}, u32[]{:S(2)}, u32[]{:S(2)}) collective-permute-start(f32[2,40,128]{2,1,0:T(8,128)S(1)} %pad_maximum_fusion), channel_id=1, source_target_pairs={{0,16},{1,17},{2,18},{3,19},{4,20},{5,21},{6,22},{7,23},{8,24},{9,... | collective-permute-start | bytes 122888 | tf_op jit(solution)/shard_map/ppermute | solution.py:421
  55.0 4.2 %collective-permute-start.10 = (f32[2,40,128]{2,1,0:T(8,128)S(1)}, f32[2,40,128]{2,1,0:T(8,128)S(1)}, u32[]{:S(2)}, u32[]{:S(2)}) collective-permute-start(f32[2,40,128]{2,1,0:T(8,128)S(1)} %pad_maximum_fusion.1), channel_id=1, source_target_pairs={{0,48},{1,49},{2,50},{3,51},{4,52},{5,53},{6,54},{7,55},{8,56},{9,... | collective-permute-start | bytes 122888 | tf_op jit(solution)/shard_map/ppermute | solution.py:421
  59.2 2.9 %collective-permute-start.11 = (f32[2,40,128]{2,1,0:T(8,128)S(1)}, f32[2,40,128]{2,1,0:T(8,128)S(1)}, u32[]{:S(2)}, u32[]{:S(2)}) collective-permute-start(f32[2,40,128]{2,1,0:T(8,128)S(1)} %pad_maximum_fusion.2), channel_id=1, source_target_pairs={{0,64},{1,65},{2,66},{3,67},{4,68},{5,69},{6,70},{7,71},{8,72},{9,... | collective-permute-start | bytes 122888 | tf_op jit(solution)/shard_map/ppermute | solution.py:421
  62.2 4.2 %collective-permute-start.12 = (f32[2,40,128]{2,1,0:T(8,128)S(1)}, f32[2,40,128]{2,1,0:T(8,128)S(1)}, u32[]{:S(2)}, u32[]{:S(2)}) collective-permute-start(f32[2,40,128]{2,1,0:T(8,128)S(1)} %pad_maximum_fusion.3), channel_id=1, source_target_pairs={{0,192},{1,193},{2,194},{3,195},{4,196},{5,197},{6,198},{7,199},{8... | collective-permute-start | bytes 122888 | tf_op jit(solution)/shard_map/ppermute | solution.py:421
  66.3 3.1 %collective-permute-start.13 = (f32[2,40,128]{2,1,0:T(8,128)S(1)}, f32[2,40,128]{2,1,0:T(8,128)S(1)}, u32[]{:S(2)}, u32[]{:S(2)}) collective-permute-start(f32[2,40,128]{2,1,0:T(8,128)S(1)} %pad_maximum_fusion.4), channel_id=1, source_target_pairs={{0,1},{1,0},{2,3},{3,2},{4,5},{5,4},{6,7},{7,6},{8,9},{9,8},{10,11... | collective-permute-start | bytes 122888 | tf_op jit(solution)/shard_map/ppermute | solution.py:421
  69.5 4.2 %collective-permute-start.14 = (f32[2,40,128]{2,1,0:T(8,128)S(1)}, f32[2,40,128]{2,1,0:T(8,128)S(1)}, u32[]{:S(2)}, u32[]{:S(2)}) collective-permute-start(f32[2,40,128]{2,1,0:T(8,128)S(1)} %pad_maximum_fusion.5), channel_id=1, source_target_pairs={{0,2},{1,3},{2,0},{3,1},{4,6},{5,7},{6,4},{7,5},{8,10},{9,11},{10,... | collective-permute-start | bytes 122888 | tf_op jit(solution)/shard_map/ppermute | solution.py:421
  73.7 5.0 %collective-permute-start.15 = (f32[2,40,128]{2,1,0:T(8,128)S(1)}, f32[2,40,128]{2,1,0:T(8,128)S(1)}, u32[]{:S(2)}, u32[]{:S(2)}) collective-permute-start(f32[2,40,128]{2,1,0:T(8,128)S(1)} %pad_maximum_fusion.6), channel_id=1, source_target_pairs={{0,6},{1,7},{2,4},{3,5},{4,2},{5,3},{6,0},{7,1},{8,14},{9,15},{10,... | collective-permute-start | bytes 122888 | tf_op jit(solution)/shard_map/ppermute | solution.py:421
  78.8 9.0 %collective-permute-start.16 = (f32[2,40,128]{2,1,0:T(8,128)S(1)}, f32[2,40,128]{2,1,0:T(8,128)S(1)}, u32[]{:S(2)}, u32[]{:S(2)}) collective-permute-start(f32[2,40,128]{2,1,0:T(8,128)S(1)} %pad_maximum_fusion.7.mine_ref), channel_id=1, source_target_pairs={{0,8},{1,9},{2,10},{3,11},{4,12},{5,13},{6,14},{7,15},{8,0},{9,1},... | collective-permute-start | bytes 122888 | tf_op jit(solution)/shard_map/ppermute | solution.py:421
where the time goes:
time: 106 us; the launch traced here: 105 us
  Pallas kernels  44.7 us (42%)
  waiting for transfers between devices  29.2 us (28%)
  starting transfers between devices  29.1 us (27%)
    ppermute x9, waiting for transfers between devices, flipped(): return lax.ppermute(value, ('gx', 'gz'), pairs)  24.9 us
    ppermute x9, starting transfers between devices, flipped(): return lax.ppermute(value, ('gx', 'gz'), pairs)  16.1 us
    ppermute x8, starting transfers between devices, shifted(): lax.ppermute(value, axis, [(i, (i + step) % count) for i in range(count)])  13 us
    pallas_call x2, Pallas kernels, criterion(): pl.pallas_call(kernel, grid=(snaps // group,), in_specs=[pl.BlockSpec((gr...  12.4 us
    pallas_call x1, Pallas kernels, factor(): pl.pallas_call(kernel, in_specs=[pl.BlockSpec(memory_space=pltpu.SMEM), v...  9.45 us
    pallas_call x1, Pallas kernels, apply_split(): pl.pallas_call(kernel, grid=(nx, halves), in_specs=[pl.BlockSpec((count,...  8.18 us
    pallas_call x2, Pallas kernels, pack_faces(): pl.pallas_call(kernel, grid=(snaps // group,), in_specs=[pl.BlockSpec(blo...  6.1 us
    pallas_call x1, Pallas kernels, gram_halves(): pl.pallas_call(kernel, grid=(steps,), in_specs=[pl.BlockSpec(memory_space...  5.58 us
  transfers between devices with their start and end apart: 17, of which 10 were waited for; matrix products, arithmetic and copies ran while one was open for 0% of the time, Pallas kernels for 12%

commit v1 on v0

--- a/solution.py
+++ b/solution.py
@@ -9,7 +9,7 @@
 precise = lax.Precision.HIGHEST
 coarse = lax.Precision.DEFAULT
 LANES = 128
-GRANT = 59 * 2**20
+GRANT = 57 * 2**20
 SPANS = ((0, 32), (32, 32))
 
 
@@ -76,7 +76,8 @@
     skip = begin // group
     halves = ny // LANES
 
-    def kernel(v_ref, lx_ref, hx_ref, lz_ref, hz_ref, out_ref, q_ref):
+    def kernel(v_ref, lx_ref, hx_ref, lz_ref, hz_ref, out_ref):
+        flat = out_ref.reshape(nx * halves * nz * group, LANES)
         lane = lax.broadcasted_iota(jnp.int32, (nz, LANES), 1)
         level = lax.broadcasted_iota(jnp.int32, (nz, LANES), 0)
 
@@ -124,28 +125,37 @@
                 for h in range(halves):
                     diagonal = dx[0][h] * dx[0][h] + dz[1][h] * dz[1][h] + dy[2][h] * dy[2][h]
                     cross = dz[0][h] * dx[1][h] + dy[0][h] * dx[2][h] + dy[1][h] * dz[2][h]
-                    q_ref[h, pl.ds((s * nx + x) * nz, nz), :] = -0.125 * diagonal - 0.25 * cross
+                    flat[pl.ds((x * halves + h) * nz * group + s, nz, stride=group), :] = -0.125 * diagonal - 0.25 * cross
             return carry
 
         lax.fori_loop(0, group, body, 0, unroll=4)
-        for x in range(nx):
-            for z in range(nz):
-                for h in range(halves):
-                    start = ((x * halves + h) * nz + z) * LANES
-                    view = q_ref.at[h]
-                    out_ref[:, start : start + LANES] = view[pl.ds(x * nz + z, group, stride=nx * nz), :]
 
     near = pl.BlockSpec(memory_space=pltpu.VMEM)
     return pl.pallas_call(
         kernel,
         grid=(snaps // group,),
         in_specs=[pl.BlockSpec((group, comps, nx, nz, ny), lambda i: (i + skip, 0, 0, 0, 0)), near, near, near, near],
-        out_specs=pl.BlockSpec((group, nx * nz * ny), lambda i: (i, 0)),
-        out_shape=jax.ShapeDtypeStruct((snaps, nx * nz * ny), velocity.dtype),
-        scratch_shapes=[pltpu.VMEM((halves, group * nx * nz, LANES), velocity.dtype)],
+        out_specs=pl.BlockSpec((1, nx * halves * nz, group, LANES), lambda i: (i, 0, 0, 0)),
+        out_shape=jax.ShapeDtypeStruct((snaps // group, nx * halves * nz, group, LANES), velocity.dtype),
         compiler_params=pltpu.CompilerParams(vmem_limit_bytes=GRANT),
         name="criterion",
     )(velocity, *[pltpu.with_memory_space_constraint(halo, pltpu.VMEM) for halo in (low_x, high_x, low_z, high_z)])
+
+
+def columns(ref, begin, count):
+    if len(ref.shape) == 2:
+        return ref[:, begin * LANES : (begin + count) * LANES]
+    return jnp.concatenate([ref[:, t].reshape(-1, LANES) for t in range(begin, begin + count)], 1)
+
+
+def rows_of(part):
+    return part.shape[0] if len(part.shape) == 2 else part.shape[0] * part.shape[2]
+
+
+def window(part, count, index):
+    if len(part.shape) == 2:
+        return pl.BlockSpec((part.shape[0], count * LANES), lambda *ids: (0, index(*ids)))
+    return pl.BlockSpec((part.shape[0], count, part.shape[2], LANES), lambda *ids: (0, index(*ids), 0, 0))
 
 
 def spread(row, shape):
@@ -308,7 +318,7 @@
 def gram_halves(parts, core, chunk=2048, piece=512):
     cells = parts[0].shape[1]
     count = len(parts)
-    size = sum(part.shape[0] for part in parts)
+    size = sum(rows_of(part) for part in parts)
     half, quarter = size // 2, size // 4
     steps = cells // chunk
 
@@ -324,8 +334,7 @@
             cross_ref[...] = jnp.zeros_like(cross_ref)
 
         for k in range(chunk // piece):
-            span = slice(k * piece, (k + 1) * piece)
-            block = jnp.concatenate([ref[:, span] for ref in part_refs], 0)
+            block = jnp.concatenate([columns(ref, k * piece // LANES, piece // LANES) for ref in part_refs], 0)
             first, second, third, _ = split(block, jnp.max(jnp.abs(block), 1, keepdims=True))
             lhs = jnp.concatenate([first, second, third], 0).astype(jnp.bfloat16)
             part = lax.dot_general(
@@ -359,7 +368,7 @@
         grid=(steps,),
         in_specs=[
             pl.BlockSpec(memory_space=pltpu.SMEM),
-            *[pl.BlockSpec((part.shape[0], chunk), lambda i: (0, i)) for part in parts],
+            *[window(part, chunk // LANES, lambda i: i) for part in parts],
         ],
         out_specs=[spec, spec],
         out_shape=[out, out],
@@ -369,7 +378,7 @@
 
 
 def apply_split(weight, parts, nx, nz, ny):
-    count = sum(part.shape[0] for part in parts)
+    count = sum(rows_of(part) for part in parts)
     halves = ny // LANES
 
     def kernel(w_ref, *refs):
@@ -383,7 +392,7 @@
             ],
             0,
         ).astype(jnp.bfloat16)
-        block = jnp.concatenate([ref[...] for ref in part_refs], 0)
+        block = jnp.concatenate([columns(ref, 0, nz) for ref in part_refs], 0)
         s1, s2, s3 = three_parts(block)
         pair = jnp.concatenate([s1, s2], 0).astype(jnp.bfloat16)
         dims = (((1,), (0,)), ((), ()))
@@ -399,7 +408,7 @@
         grid=(nx, halves),
         in_specs=[
             pl.BlockSpec((count, count), lambda i, h: (0, 0)),
-            *[pl.BlockSpec((part.shape[0], nz * LANES), lambda i, h: (0, i * halves + h)) for part in parts],
+            *[window(part, nz, lambda i, h: i * halves + h) for part in parts],
         ],
         out_specs=pl.BlockSpec((count, 1, nz, LANES), lambda i, h: (0, i, 0, h)),
         out_shape=jax.ShapeDtypeStruct((count, nx, nz, ny), jnp.float32),

time: 106 us -> 106 us (level)
  Pallas kernels: 44.7 us -> 43.5 us
    pallas_call x2, Pallas kernels: 12.4 us -> 11.2 us  [criterion(): pl.pallas_call(kernel, grid=(snaps // group,), in_specs=[pl.BlockSpec((gr...]
  transfers between devices with their start and end apart: 17 -> 17, of which waited for: 10 -> 10; matrix products, arithmetic and copies ran while one was open for 0% -> 0% of each run, Pallas kernels for 12% -> 11%
where the time goes in v1:
time: 106 us; the launch traced here: 105 us
  Pallas kernels  43.5 us (41%)
  waiting for transfers between devices  29.2 us (28%)
  starting transfers between devices  29 us (27%)
  local copies, waits for them, and re-layouts  1.74 us (2%)
    ppermute x9, waiting for transfers between devices, flipped(): return lax.ppermute(value, ('gx', 'gz'), pairs)  25 us
    ppermute x9, starting transfers between devices, flipped(): return lax.ppermute(value, ('gx', 'gz'), pairs)  16.1 us
    ppermute x8, starting transfers between devices, shifted(): lax.ppermute(value, axis, [(i, (i + step) % count) for i in range(count)])  12.9 us
    pallas_call x2, Pallas kernels, criterion(): pl.pallas_call(kernel, grid=(snaps // group,), in_specs=[pl.BlockSpec((gr...  11.2 us
    pallas_call x1, Pallas kernels, factor(): pl.pallas_call(kernel, in_specs=[pl.BlockSpec(memory_space=pltpu.SMEM), v...  9.45 us
    pallas_call x1, Pallas kernels, apply_split(): pl.pallas_call(kernel, grid=(nx, halves), in_specs=[pl.BlockSpec((count,...  8.12 us
    pallas_call x2, Pallas kernels, pack_faces(): pl.pallas_call(kernel, grid=(snaps // group,), in_specs=[pl.BlockSpec(blo...  6.12 us
    pallas_call x1, Pallas kernels, gram_halves(): pl.pallas_call(kernel, grid=(steps,), in_specs=[pl.BlockSpec(memory_space...  5.59 us
  transfers between devices with their start and end apart: 17, of which 10 were waited for; matrix products, arithmetic and copies ran while one was open for 0% of the time, Pallas kernels for 11%

profile of v1, /device:TPU:1, one launch (start us, length us, event | category | flops | bytes accessed | tf_op | source)
XLA Modules:
  0.0 105.2 jit_solution(3315958643519935189)
XLA Ops:
  0.6 3.0 %pack_faces.2 = (f32[32,3,8,256]{3,2,1,0:T(8,128)}, f32[32,3,8,256]{3,2,1,0:T(8,128)}, f32[2,384,128]{2,1,0:T(8,128)}, f32[2,384,128]{2,1,0:T(8,128)}) custom-call(f32[64,3,4,8,256]{4,3,2,1,0:T(8,128)} %v_ref.3, f32[64,3,4,8,256]{4,3,2,1,0:T(8,128)} %v_ref.3), custom_call_target="tpu_custom_call" | custom-call | tf_op jit(solution)/shard_map/pack_faces/pallas_call | solution.py:37
  3.6 2.6 %collective-permute-start = (f32[32,3,8,256]{3,2,1,0:T(8,128)}, f32[32,3,8,256]{3,2,1,0:T(8,128)S(1)}, u32[]{:S(2)}, u32[]{:S(2)}) collective-permute-start(f32[32,3,8,256]{3,2,1,0:T(8,128)} %get-tuple-element.16), channel_id=1, source_target_pairs={{0,8},{8,16},{16,24},{24,32},{32,40},{40,48},{48,56},{56,64},{64,7... | collective-permute-start | bytes 2359304 | tf_op jit(solution)/shard_map/ppermute | solution.py:422
  6.2 1.6 %collective-permute-start.2 = (f32[2,384,128]{2,1,0:T(8,128)}, f32[2,384,128]{2,1,0:T(8,128)S(1)}, u32[]{:S(2)}, u32[]{:S(2)}) collective-permute-start(f32[2,384,128]{2,1,0:T(8,128)} %get-tuple-element.18), channel_id=1, source_target_pairs={{0,1},{1,2},{2,3},{3,4},{4,5},{5,6},{6,7},{7,0},{8,9},{9,10},{10,1... | collective-permute-start | bytes 1179656 | tf_op jit(solution)/shard_map/ppermute | solution.py:422
  7.9 3.9 %collective-permute-start.3 = (f32[2,384,128]{2,1,0:T(8,128)}, f32[2,384,128]{2,1,0:T(8,128)S(1)}, u32[]{:S(2)}, u32[]{:S(2)}) collective-permute-start(f32[2,384,128]{2,1,0:T(8,128)} %get-tuple-element.19), channel_id=1, source_target_pairs={{0,7},{1,0},{2,1},{3,2},{4,3},{5,4},{6,5},{7,6},{8,15},{9,8},{10,9... | collective-permute-start | bytes 1179656 | tf_op jit(solution)/shard_map/ppermute | solution.py:422
  11.8 3.1 %pack_faces.3 = (f32[32,3,8,256]{3,2,1,0:T(8,128)}, f32[32,3,8,256]{3,2,1,0:T(8,128)}, f32[2,384,128]{2,1,0:T(8,128)}, f32[2,384,128]{2,1,0:T(8,128)}) custom-call(f32[64,3,4,8,256]{4,3,2,1,0:T(8,128)} %v_ref.3, f32[64,3,4,8,256]{4,3,2,1,0:T(8,128)} %v_ref.3), custom_call_target="tpu_custom_call" | custom-call | tf_op jit(solution)/shard_map/pack_faces/pallas_call | solution.py:37
  14.9 1.7 %collective-permute-start.4 = (f32[32,3,8,256]{3,2,1,0:T(8,128)}, f32[32,3,8,256]{3,2,1,0:T(8,128)S(1)}, u32[]{:S(2)}, u32[]{:S(2)}) collective-permute-start(f32[32,3,8,256]{3,2,1,0:T(8,128)} %get-tuple-element.20), channel_id=1, source_target_pairs={{0,8},{8,16},{16,24},{24,32},{32,40},{40,48},{48,56},{56,64},{64,7... | collective-permute-start | bytes 2359304 | tf_op jit(solution)/shard_map/ppermute | solution.py:422
  16.6 4.2 %collective-permute-done.2.lz_ref = f32[2,384,128]{2,1,0:T(8,128)S(1)} collective-permute-done((f32[2,384,128]{2,1,0:T(8,128)}, f32[2,384,128]{2,1,0:T(8,128)S(1)}, u32[]{:S(2)}, u32[]{:S(2)}) %collective-permute-start.2) | collective-permute-done | bytes 393248 | tf_op jit(solution)/shard_map/ppermute | solution.py:422
  20.9 0.7 copy-done
  21.6 3.0 %collective-permute-start.7 = (f32[2,384,128]{2,1,0:T(8,128)}, f32[2,384,128]{2,1,0:T(8,128)}, u32[]{:S(2)}, u32[]{:S(2)}) collective-permute-start(f32[2,384,128]{2,1,0:T(8,128)} %get-tuple-element.23), channel_id=1, source_target_pairs={{0,7},{1,0},{2,1},{3,2},{4,3},{5,4},{6,5},{7,6},{8,15},{9,8},{10,9... | collective-permute-start | bytes 1179656 | tf_op jit(solution)/shard_map/ppermute | solution.py:422
  24.7 3.0 %flatten_modes.1.refs_0_ = f32[64,8192]{1,0:T(8,128)} custom-call(f32[64,4,8,256]{3,2,1,0:T(8,128)} %refs_1_.3, f32[64,4,8,256]{3,2,1,0:T(8,128)} %refs_1_.3), custom_call_target="tpu_custom_call" | custom-call | tf_op jit(solution)/shard_map/flatten_modes/pallas_call | solution.py:62
  27.7 1.0 copy-done.1
  28.6 5.5 %criterion.2.refs_1_ = f32[4,64,8,128]{3,2,1,0:T(8,128)} custom-call(f32[64,3,4,8,256]{4,3,2,1,0:T(8,128)} %v_ref.3, f32[32,3,8,256]{3,2,1,0:T(8,128)S(1)} %collective-permute-done.lx_ref, f32[32,3,8,256]{3,2,1,0:T(8,128)S(1)} %collective-permute-done.1.hx_ref, f32[2,384,128]{2,1,0:T(8,128)S(1)} %collective-permute-done.2.lz_ref, f32[2,384,128]{2,1,0:T(8,128)S(1)} %copy-done.1), custom_call_target="tpu_custom_call" | custom-call | tf_op jit(solution)/shard_map/criterion/pallas_call | solution.py:134
  34.2 5.8 %criterion.3.refs_2_ = f32[4,64,8,128]{3,2,1,0:T(8,128)} custom-call(f32[64,3,4,8,256]{4,3,2,1,0:T(8,128)} %v_ref.3, f32[32,3,8,256]{3,2,1,0:T(8,128)S(1)} %collective-permute-done.4.lx_ref, f32[32,3,8,256]{3,2,1,0:T(8,128)S(1)} %collective-permute-done.5.hx_ref, f32[2,384,128]{2,1,0:T(8,128)} %collective-permute-done.6.lz_ref, ...), custom_call_target="tpu_custom_call" | custom-call | tf_op jit(solution)/shard_map/criterion/pallas_call | solution.py:134
  39.9 5.6 %gram_halves.1 = (f32[2,40,128]{2,1,0:T(8,128)}, f32[2,40,128]{2,1,0:T(8,128)}) custom-call(s32[1]{0:T(128)} %bitcast.core_ref, f32[64,8192]{1,0:T(8,128)} %flatten_modes.1.refs_0_, f32[4,64,8,128]{3,2,1,0:T(8,128)} %criterion.2.refs_1_, f32[4,64,8,128]{3,2,1,0:T(8,128)} %criterion.3.refs_2_), custom_call_target="tpu_custom_call" | custom-call | tf_op jit(solution)/shard_map/gram_halves/pallas_call | solution.py:366
  45.5 4.5 %collective-permute-start.8 = (f32[2,40,128]{2,1,0:T(8,128)}, f32[2,40,128]{2,1,0:T(8,128)S(1)}, u32[]{:S(2)}, u32[]{:S(2)}) collective-permute-start(f32[2,40,128]{2,1,0:T(8,128)} %get-tuple-element.25), channel_id=1, source_target_pairs={{0,8},{1,9},{2,10},{3,11},{4,12},{5,13},{6,14},{7,15},{8,0},{9,1},... | collective-permute-start | bytes 122888 | tf_op jit(solution)/shard_map/ppermute | solution.py:430
  50.0 1.1 %collective-permute-done.8 = f32[2,40,128]{2,1,0:T(8,128)S(1)} collective-permute-done((f32[2,40,128]{2,1,0:T(8,128)}, f32[2,40,128]{2,1,0:T(8,128)S(1)}, u32[]{:S(2)}, u32[]{:S(2)}) %collective-permute-start.8) | collective-permute-done | bytes 40992 | tf_op jit(solution)/shard_map/ppermute | solution.py:430
  51.1 0.8 fusion.7
  51.9 2.8 %collective-permute-done.9 = f32[2,40,128]{2,1,0:T(8,128)S(1)} collective-permute-done((f32[2,40,128]{2,1,0:T(8,128)S(1)}, f32[2,40,128]{2,1,0:T(8,128)S(1)}, u32[]{:S(2)}, u32[]{:S(2)}) %collective-permute-start.9) | collective-permute-done | bytes 40992 | tf_op jit(solution)/shard_map/ppermute | solution.py:430
  54.9 4.0 %collective-permute-done.10 = f32[2,40,128]{2,1,0:T(8,128)S(1)} collective-permute-done((f32[2,40,128]{2,1,0:T(8,128)S(1)}, f32[2,40,128]{2,1,0:T(8,128)S(1)}, u32[]{:S(2)}, u32[]{:S(2)}) %collective-permute-start.10) | collective-permute-done | bytes 40992 | tf_op jit(solution)/shard_map/ppermute | solution.py:430
  59.1 2.8 %collective-permute-done.11 = f32[2,40,128]{2,1,0:T(8,128)S(1)} collective-permute-done((f32[2,40,128]{2,1,0:T(8,128)S(1)}, f32[2,40,128]{2,1,0:T(8,128)S(1)}, u32[]{:S(2)}, u32[]{:S(2)}) %collective-permute-start.11) | collective-permute-done | bytes 40992 | tf_op jit(solution)/shard_map/ppermute | solution.py:430
  62.0 1.3 %collective-permute-start.12 = (f32[2,40,128]{2,1,0:T(8,128)S(1)}, f32[2,40,128]{2,1,0:T(8,128)S(1)}, u32[]{:S(2)}, u32[]{:S(2)}) collective-permute-start(f32[2,40,128]{2,1,0:T(8,128)S(1)} %pad_maximum_fusion.3), channel_id=1, source_target_pairs={{0,192},{1,193},{2,194},{3,195},{4,196},{5,197},{6,198},{7,199},{8... | collective-permute-start | bytes 122888 | tf_op jit(solution)/shard_map/ppermute | solution.py:430
  63.3 2.9 %collective-permute-done.12 = f32[2,40,128]{2,1,0:T(8,128)S(1)} collective-permute-done((f32[2,40,128]{2,1,0:T(8,128)S(1)}, f32[2,40,128]{2,1,0:T(8,128)S(1)}, u32[]{:S(2)}, u32[]{:S(2)}) %collective-permute-start.12) | collective-permute-done | bytes 40992 | tf_op jit(solution)/shard_map/ppermute | solution.py:430
  66.1 0.1 collective-permute-start.13
  66.2 2.8 %collective-permute-done.13 = f32[2,40,128]{2,1,0:T(8,128)S(1)} collective-permute-done((f32[2,40,128]{2,1,0:T(8,128)S(1)}, f32[2,40,128]{2,1,0:T(8,128)S(1)}, u32[]{:S(2)}, u32[]{:S(2)}) %collective-permute-start.13) | collective-permute-done | bytes 40992 | tf_op jit(solution)/shard_map/ppermute | solution.py:430
  69.1 0.3 collective-permute-start.14
  69.4 4.0 %collective-permute-done.14 = f32[2,40,128]{2,1,0:T(8,128)S(1)} collective-permute-done((f32[2,40,128]{2,1,0:T(8,128)S(1)}, f32[2,40,128]{2,1,0:T(8,128)S(1)}, u32[]{:S(2)}, u32[]{:S(2)}) %collective-permute-start.14) | collective-permute-done | bytes 40992 | tf_op jit(solution)/shard_map/ppermute | solution.py:430
  73.4 1.5 %collective-permute-start.15 = (f32[2,40,128]{2,1,0:T(8,128)S(1)}, f32[2,40,128]{2,1,0:T(8,128)S(1)}, u32[]{:S(2)}, u32[]{:S(2)}) collective-permute-start(f32[2,40,128]{2,1,0:T(8,128)S(1)} %pad_maximum_fusion.6), channel_id=1, source_target_pairs={{0,6},{1,7},{2,4},{3,5},{4,2},{5,3},{6,0},{7,1},{8,14},{9,15},{10,... | collective-permute-start | bytes 122888 | tf_op jit(solution)/shard_map/ppermute | solution.py:430
  74.9 3.6 %collective-permute-done.15 = f32[2,40,128]{2,1,0:T(8,128)S(1)} collective-permute-done((f32[2,40,128]{2,1,0:T(8,128)S(1)}, f32[2,40,128]{2,1,0:T(8,128)S(1)}, u32[]{:S(2)}, u32[]{:S(2)}) %collective-permute-start.15) | collective-permute-done | bytes 40992 | tf_op jit(solution)/shard_map/ppermute | solution.py:430
  78.5 8.2 %collective-permute-start.16 = (f32[2,40,128]{2,1,0:T(8,128)S(1)}, f32[2,40,128]{2,1,0:T(8,128)S(1)}, u32[]{:S(2)}, u32[]{:S(2)}) collective-permute-start(f32[2,40,128]{2,1,0:T(8,128)S(1)} %pad_maximum_fusion.7.mine_ref), channel_id=1, source_target_pairs={{0,8},{1,9},{2,10},{3,11},{4,12},{5,13},{6,14},{7,15},{8,0},{9,1},... | collective-permute-start | bytes 122888 | tf_op jit(solution)/shard_map/ppermute | solution.py:430
  86.7 0.9 collective-permute-done.16.other_ref
  87.6 9.5 %factor.1 = (f32[128,128]{1,0:T(8,128)}, f32[128,128]{1,0:T(8,128)}, f32[128,128]{1,0:T(8,128)}) custom-call(s32[1]{0:T(128)} %bitcast.core_ref, f32[2,40,128]{2,1,0:T(8,128)S(1)} %pad_maximum_fusion.7.mine_ref, f32[2,40,128]{2,1,0:T(8,128)S(1)} %collective-permute-done.16.other_ref), custom_call_target="tpu_custom_call" | custom-call | tf_op jit(solution)/shard_map/factor/pallas_call | solution.py:298
  97.0 8.1 %apply_split.1 = f32[128,4,8,256]{3,2,1,0:T(8,128)} custom-call(f32[128,128]{1,0:T(8,128)} %get-tuple-element.26.w_ref, f32[64,8192]{1,0:T(8,128)} %flatten_modes.1.refs_0_, f32[4,64,8,128]{3,2,1,0:T(8,128)} %criterion.2.refs_1_, f32[4,64,8,128]{3,2,1,0:T(8,128)} %criterion.3.refs_2_), custom_call_target="tpu_custom_call" | custom-call | tf_op jit(solution)/shard_map/apply_split/pallas_call | solution.py:406
  (30 shorter events, 0.4 us)
Async XLA Ops:
  3.6 18.0 %collective-permute-start = (f32[32,3,8,256]{3,2,1,0:T(8,128)}, f32[32,3,8,256]{3,2,1,0:T(8,128)S(1)}, u32[]{:S(2)}, u32[]{:S(2)}) collective-permute-start(f32[32,3,8,256]{3,2,1,0:T(8,128)} %get-tuple-element.16), channel_id=1, source_target_pairs={{0,8},{8,16},{16,24},{24,32},{32,40},{40,48},{48,56},{56,64},{64,7... | collective-permute-start | bytes 2359304 | tf_op jit(solution)/shard_map/ppermute | solution.py:422
  6.2 14.6 %collective-permute-start.2 = (f32[2,384,128]{2,1,0:T(8,128)}, f32[2,384,128]{2,1,0:T(8,128)S(1)}, u32[]{:S(2)}, u32[]{:S(2)}) collective-permute-start(f32[2,384,128]{2,1,0:T(8,128)} %get-tuple-element.18), channel_id=1, source_target_pairs={{0,1},{1,2},{2,3},{3,4},{4,5},{5,6},{6,7},{7,0},{8,9},{9,10},{10,1... | collective-permute-start | bytes 1179656 | tf_op jit(solution)/shard_map/ppermute | solution.py:422
  7.9 13.0 %collective-permute-start.3 = (f32[2,384,128]{2,1,0:T(8,128)}, f32[2,384,128]{2,1,0:T(8,128)S(1)}, u32[]{:S(2)}, u32[]{:S(2)}) collective-permute-start(f32[2,384,128]{2,1,0:T(8,128)} %get-tuple-element.19), channel_id=1, source_target_pairs={{0,7},{1,0},{2,1},{3,2},{4,3},{5,4},{6,5},{7,6},{8,15},{9,8},{10,9... | collective-permute-start | bytes 1179656 | tf_op jit(solution)/shard_map/ppermute | solution.py:422
  11.8 15.8 %collective-permute-start.1 = (f32[32,3,8,256]{3,2,1,0:T(8,128)}, f32[32,3,8,256]{3,2,1,0:T(8,128)S(1)}, u32[]{:S(2)}, u32[]{:S(2)}) collective-permute-start(f32[32,3,8,256]{3,2,1,0:T(8,128)} %get-tuple-element.17), channel_id=1, source_target_pairs={{0,248},{8,0},{16,8},{24,16},{32,24},{40,32},{48,40},{56,48},{64,5... | collective-permute-start | bytes 2359304 | tf_op jit(solution)/shard_map/ppermute | solution.py:422
  14.9 19.2 %collective-permute-start.4 = (f32[32,3,8,256]{3,2,1,0:T(8,128)}, f32[32,3,8,256]{3,2,1,0:T(8,128)S(1)}, u32[]{:S(2)}, u32[]{:S(2)}) collective-permute-start(f32[32,3,8,256]{3,2,1,0:T(8,128)} %get-tuple-element.20), channel_id=1, source_target_pairs={{0,8},{8,16},{16,24},{24,32},{32,40},{40,48},{48,56},{56,64},{64,7... | collective-permute-start | bytes 2359304 | tf_op jit(solution)/shard_map/ppermute | solution.py:422
  20.9 13.3 %collective-permute-start.5 = (f32[32,3,8,256]{3,2,1,0:T(8,128)}, f32[32,3,8,256]{3,2,1,0:T(8,128)S(1)}, u32[]{:S(2)}, u32[]{:S(2)}) collective-permute-start(f32[32,3,8,256]{3,2,1,0:T(8,128)} %get-tuple-element.21), channel_id=1, source_target_pairs={{0,248},{8,0},{16,8},{24,16},{32,24},{40,32},{48,40},{56,48},{64,5... | collective-permute-start | bytes 2359304 | tf_op jit(solution)/shard_map/ppermute | solution.py:422
  20.9 0.7 copy-start
  21.6 12.5 %collective-permute-start.6 = (f32[2,384,128]{2,1,0:T(8,128)}, f32[2,384,128]{2,1,0:T(8,128)}, u32[]{:S(2)}, u32[]{:S(2)}) collective-permute-start(f32[2,384,128]{2,1,0:T(8,128)} %get-tuple-element.22), channel_id=1, source_target_pairs={{0,1},{1,2},{2,3},{3,4},{4,5},{5,6},{6,7},{7,0},{8,9},{9,10},{10,1... | collective-permute-start | bytes 1179656 | tf_op jit(solution)/shard_map/ppermute | solution.py:422
  21.6 12.5 %collective-permute-start.7 = (f32[2,384,128]{2,1,0:T(8,128)}, f32[2,384,128]{2,1,0:T(8,128)}, u32[]{:S(2)}, u32[]{:S(2)}) collective-permute-start(f32[2,384,128]{2,1,0:T(8,128)} %get-tuple-element.23), channel_id=1, source_target_pairs={{0,7},{1,0},{2,1},{3,2},{4,3},{5,4},{6,5},{7,6},{8,15},{9,8},{10,9... | collective-permute-start | bytes 1179656 | tf_op jit(solution)/shard_map/ppermute | solution.py:422
  27.7 1.0 copy-start.1
  45.5 5.6 %collective-permute-start.8 = (f32[2,40,128]{2,1,0:T(8,128)}, f32[2,40,128]{2,1,0:T(8,128)S(1)}, u32[]{:S(2)}, u32[]{:S(2)}) collective-permute-start(f32[2,40,128]{2,1,0:T(8,128)} %get-tuple-element.25), channel_id=1, source_target_pairs={{0,8},{1,9},{2,10},{3,11},{4,12},{5,13},{6,14},{7,15},{8,0},{9,1},... | collective-permute-start | bytes 122888 | tf_op jit(solution)/shard_map/ppermute | solution.py:430
  51.8 2.9 %collective-permute-start.9 = (f32[2,40,128]{2,1,0:T(8,128)S(1)}, f32[2,40,128]{2,1,0:T(8,128)S(1)}, u32[]{:S(2)}, u32[]{:S(2)}) collective-permute-start(f32[2,40,128]{2,1,0:T(8,128)S(1)} %pad_maximum_fusion), channel_id=1, source_target_pairs={{0,16},{1,17},{2,18},{3,19},{4,20},{5,21},{6,22},{7,23},{8,24},{9,... | collective-permute-start | bytes 122888 | tf_op jit(solution)/shard_map/ppermute | solution.py:430
  54.8 4.2 %collective-permute-start.10 = (f32[2,40,128]{2,1,0:T(8,128)S(1)}, f32[2,40,128]{2,1,0:T(8,128)S(1)}, u32[]{:S(2)}, u32[]{:S(2)}) collective-permute-start(f32[2,40,128]{2,1,0:T(8,128)S(1)} %pad_maximum_fusion.1), channel_id=1, source_target_pairs={{0,48},{1,49},{2,50},{3,51},{4,52},{5,53},{6,54},{7,55},{8,56},{9,... | collective-permute-start | bytes 122888 | tf_op jit(solution)/shard_map/ppermute | solution.py:430
  59.0 2.9 %collective-permute-start.11 = (f32[2,40,128]{2,1,0:T(8,128)S(1)}, f32[2,40,128]{2,1,0:T(8,128)S(1)}, u32[]{:S(2)}, u32[]{:S(2)}) collective-permute-start(f32[2,40,128]{2,1,0:T(8,128)S(1)} %pad_maximum_fusion.2), channel_id=1, source_target_pairs={{0,64},{1,65},{2,66},{3,67},{4,68},{5,69},{6,70},{7,71},{8,72},{9,... | collective-permute-start | bytes 122888 | tf_op jit(solution)/shard_map/ppermute | solution.py:430
  62.0 4.2 %collective-permute-start.12 = (f32[2,40,128]{2,1,0:T(8,128)S(1)}, f32[2,40,128]{2,1,0:T(8,128)S(1)}, u32[]{:S(2)}, u32[]{:S(2)}) collective-permute-start(f32[2,40,128]{2,1,0:T(8,128)S(1)} %pad_maximum_fusion.3), channel_id=1, source_target_pairs={{0,192},{1,193},{2,194},{3,195},{4,196},{5,197},{6,198},{7,199},{8... | collective-permute-start | bytes 122888 | tf_op jit(solution)/shard_map/ppermute | solution.py:430
  66.1 2.9 %collective-permute-start.13 = (f32[2,40,128]{2,1,0:T(8,128)S(1)}, f32[2,40,128]{2,1,0:T(8,128)S(1)}, u32[]{:S(2)}, u32[]{:S(2)}) collective-permute-start(f32[2,40,128]{2,1,0:T(8,128)S(1)} %pad_maximum_fusion.4), channel_id=1, source_target_pairs={{0,1},{1,0},{2,3},{3,2},{4,5},{5,4},{6,7},{7,6},{8,9},{9,8},{10,11... | collective-permute-start | bytes 122888 | tf_op jit(solution)/shard_map/ppermute | solution.py:430
  69.1 4.3 %collective-permute-start.14 = (f32[2,40,128]{2,1,0:T(8,128)S(1)}, f32[2,40,128]{2,1,0:T(8,128)S(1)}, u32[]{:S(2)}, u32[]{:S(2)}) collective-permute-start(f32[2,40,128]{2,1,0:T(8,128)S(1)} %pad_maximum_fusion.5), channel_id=1, source_target_pairs={{0,2},{1,3},{2,0},{3,1},{4,6},{5,7},{6,4},{7,5},{8,10},{9,11},{10,... | collective-permute-start | bytes 122888 | tf_op jit(solution)/shard_map/ppermute | solution.py:430
  73.4 5.0 %collective-permute-start.15 = (f32[2,40,128]{2,1,0:T(8,128)S(1)}, f32[2,40,128]{2,1,0:T(8,128)S(1)}, u32[]{:S(2)}, u32[]{:S(2)}) collective-permute-start(f32[2,40,128]{2,1,0:T(8,128)S(1)} %pad_maximum_fusion.6), channel_id=1, source_target_pairs={{0,6},{1,7},{2,4},{3,5},{4,2},{5,3},{6,0},{7,1},{8,14},{9,15},{10,... | collective-permute-start | bytes 122888 | tf_op jit(solution)/shard_map/ppermute | solution.py:430
  78.5 9.1 %collective-permute-start.16 = (f32[2,40,128]{2,1,0:T(8,128)S(1)}, f32[2,40,128]{2,1,0:T(8,128)S(1)}, u32[]{:S(2)}, u32[]{:S(2)}) collective-permute-start(f32[2,40,128]{2,1,0:T(8,128)S(1)} %pad_maximum_fusion.7.mine_ref), channel_id=1, source_target_pairs={{0,8},{1,9},{2,10},{3,11},{4,12},{5,13},{6,14},{7,15},{8,0},{9,1},... | collective-permute-start | bytes 122888 | tf_op jit(solution)/shard_map/ppermute | solution.py:430

commit v2 on v1

--- a/solution.py
+++ b/solution.py
@@ -45,29 +45,47 @@
     )(*[velocity] * halves)
 
 
-def flatten_modes(modes, group=2):
+def flatten_modes(modes, piece=512):
     count, nx, nz, ny = modes.shape
     halves = ny // LANES
-
-    def kernel(*refs):
-        out_ref = refs[halves]
-        for h in range(halves):
-            flat = refs[h].reshape(count * group * nz, LANES)
-            for x in range(group):
-                for z in range(nz):
-                    start = ((x * halves + h) * nz + z) * LANES
-                    out_ref[:, start : start + LANES] = flat[pl.ds(x * nz + z, count, stride=group * nz), :]
-
-    block = (count, group, nz, LANES)
+    width = nx * nz * LANES
+
+    def kernel(m_ref, out_ref, gram_ref):
+
+        @pl.when(pl.program_id(0) == 0)
+        def _():
+            gram_ref[...] = jnp.zeros_like(gram_ref)
+
+        flat = m_ref.reshape(count * nx * nz, LANES)
+        for t in range(nx * nz):
+            out_ref[:, t * LANES : (t + 1) * LANES] = flat[pl.ds(t, count, stride=nx * nz), :]
+        for k in range(width // piece):
+            block = out_ref[:, k * piece : (k + 1) * piece]
+            first, second, third, _ = split(block, jnp.max(jnp.abs(block), 1, keepdims=True))
+            lhs = jnp.concatenate([first, second, third], 0).astype(jnp.bfloat16)
+            part = lax.dot_general(
+                lhs, lhs[: 2 * count], (((1,), (1,)), ((), ())), preferred_element_type=jnp.float32
+            )
+            middle, last = part[count : 2 * count], part[2 * count :]
+            gram_ref[0], error = two_sum(gram_ref[0], part[:count])
+            gram_ref[1] += error + pltpu.roll(middle, count, 1)
+            gram_ref[2] += middle + (last + pltpu.roll(last, count, 1))
+
     return pl.pallas_call(
         kernel,
-        grid=(nx // group,),
-        in_specs=[pl.BlockSpec(block, lambda i, h=h: (0, i, 0, h)) for h in range(halves)],
-        out_specs=pl.BlockSpec((count, group * nz * ny), lambda i: (0, i)),
-        out_shape=jax.ShapeDtypeStruct((count, nx * nz * ny), modes.dtype),
+        grid=(halves,),
+        in_specs=[pl.BlockSpec((count, nx, nz, LANES), lambda h: (0, 0, 0, h))],
+        out_specs=[
+            pl.BlockSpec((count, width), lambda i: (0, i)),
+            pl.BlockSpec((3, count, 2 * count), lambda i: (0, 0, 0)),
+        ],
+        out_shape=[
+            jax.ShapeDtypeStruct((count, nx * nz * ny), modes.dtype),
+            jax.ShapeDtypeStruct((3, count, 2 * count), jnp.float32),
+        ],
         compiler_params=pltpu.CompilerParams(vmem_limit_bytes=GRANT),
         name="flatten_modes",
-    )(*[modes] * halves)
+    )(modes)
 
 
 def criterion(velocity, low_x, high_x, low_z, high_z, begin, group=8):
@@ -125,7 +143,7 @@
                 for h in range(halves):
                     diagonal = dx[0][h] * dx[0][h] + dz[1][h] * dz[1][h] + dy[2][h] * dy[2][h]
                     cross = dz[0][h] * dx[1][h] + dy[0][h] * dx[2][h] + dy[1][h] * dz[2][h]
-                    flat[pl.ds((x * halves + h) * nz * group + s, nz, stride=group), :] = -0.125 * diagonal - 0.25 * cross
+                    flat[pl.ds((h * nx + x) * nz * group + s, nz, stride=group), :] = -0.125 * diagonal - 0.25 * cross
             return carry
 
         lax.fori_loop(0, group, body, 0, unroll=4)
@@ -315,7 +333,7 @@
     return total, (left - (total - back)) + (right - back)
 
 
-def gram_halves(parts, core, chunk=2048, piece=512):
+def gram_halves(parts, own, core, chunk=2048, piece=512):
     cells = parts[0].shape[1]
     count = len(parts)
     size = sum(rows_of(part) for part in parts)
@@ -324,30 +342,40 @@
 
     def kernel(core_ref, *refs):
         part_refs = refs[:count]
-        keep_ref, send_ref, high_ref, low_ref, cross_ref = refs[count:]
+        own_ref, keep_ref, send_ref, high_ref, low_ref, cross_ref = refs[count:]
+        side = lax.broadcasted_iota(jnp.int32, (half, size), 1) < half
         step = pl.program_id(0)
 
         @pl.when(step == 0)
         def _():
-            high_ref[...] = jnp.zeros_like(high_ref)
-            low_ref[...] = jnp.zeros_like(low_ref)
-            cross_ref[...] = jnp.zeros_like(cross_ref)
+            high_ref[half:] = jnp.zeros((half, size), jnp.float32)
+            low_ref[half:] = jnp.zeros((half, size), jnp.float32)
+            cross_ref[half:] = jnp.zeros((half, size), jnp.float32)
+            high_ref[:half] = own_ref[0]
+            low_ref[:half] = own_ref[1]
+            cross_ref[:half] = jnp.where(side, own_ref[2], 0.0)
 
         for k in range(chunk // piece):
             block = jnp.concatenate([columns(ref, k * piece // LANES, piece // LANES) for ref in part_refs], 0)
             first, second, third, _ = split(block, jnp.max(jnp.abs(block), 1, keepdims=True))
-            lhs = jnp.concatenate([first, second, third], 0).astype(jnp.bfloat16)
-            part = lax.dot_general(
-                lhs, lhs[: 2 * size], (((1,), (1,)), ((), ())), preferred_element_type=jnp.float32
-            )
-            high_ref[...], error = two_sum(high_ref[...], part[:size, :size])
-            low_ref[...] += error + part[size : 2 * size, size:]
-            cross_ref[...] += part[size : 2 * size, :size] + (part[2 * size :, :size] + part[2 * size :, size:])
+            lhs = jnp.concatenate([first[half:], second[half:], third[half:], third[:half]], 0).astype(jnp.bfloat16)
+            rhs = jnp.concatenate([first, second], 0).astype(jnp.bfloat16)
+            part = lax.dot_general(lhs, rhs, (((1,), (1,)), ((), ())), preferred_element_type=jnp.float32)
+            top, middle, last = part[:half], part[half : 2 * half], part[2 * half : 3 * half]
+            high_ref[half:], error = two_sum(high_ref[half:], top[:, :size])
+            low_ref[half:] += error + middle[:, size:]
+            cross_ref[half:] += (jnp.where(side, top[:, size:], 0.0) + middle[:, :size]) + (last[:, :size] + last[:, size:])
+            cross_ref[:half] += jnp.where(side, 0.0, part[3 * half :, :size])
 
         @pl.when(step == steps - 1)
         def _():
             cross = cross_ref[...]
-            high_ref[...], low_ref[...] = two_sum(high_ref[...], low_ref[...] + (cross + cross.T))
+            high, low = two_sum(high_ref[...], low_ref[...] + (cross + cross.T))
+            square_row = lax.broadcasted_iota(jnp.int32, (size, size), 0)
+            square_lane = lax.broadcasted_iota(jnp.int32, (size, size), 1)
+            mixed = jnp.logical_and(square_row < half, square_lane >= half)
+            high_ref[...] = jnp.where(mixed, high.T, high)
+            low_ref[...] = jnp.where(mixed, low.T, low)
             lane = lax.broadcasted_iota(jnp.int32, (half, size), 1)
             row = lax.broadcasted_iota(jnp.int32, (half, size), 0)
             lead = core_ref[0] == 0
@@ -361,7 +389,7 @@
                 keep_ref[k] = jnp.where(lead, low, high)
                 send_ref[k] = jnp.where(lead, high, low)
 
-    out = jax.ShapeDtypeStruct((2, quarter + 8, size), jnp.float32)
+    out = pltpu.VMEM((2, quarter + 8, size), jnp.float32)
     spec = pl.BlockSpec((2, quarter + 8, size), lambda i: (0, 0, 0))
     return pl.pallas_call(
         kernel,
@@ -369,15 +397,16 @@
         in_specs=[
             pl.BlockSpec(memory_space=pltpu.SMEM),
             *[window(part, chunk // LANES, lambda i: i) for part in parts],
+            pl.BlockSpec((3, half, size), lambda i: (0, 0, 0)),
         ],
         out_specs=[spec, spec],
         out_shape=[out, out],
         scratch_shapes=[pltpu.VMEM((size, size), jnp.float32)] * 3,
         name="gram_halves",
-    )(core, *parts)
-
-
-def apply_split(weight, parts, nx, nz, ny):
+    )(core, *parts, own)
+
+
+def apply_split(weight, parts, nx, nz, ny, group=2):
     count = sum(rows_of(part) for part in parts)
     halves = ny // LANES
 
@@ -392,25 +421,28 @@
             ],
             0,
         ).astype(jnp.bfloat16)
-        block = jnp.concatenate([columns(ref, 0, nz) for ref in part_refs], 0)
-        s1, s2, s3 = three_parts(block)
-        pair = jnp.concatenate([s1, s2], 0).astype(jnp.bfloat16)
         dims = (((1,), (0,)), ((), ()))
-        main = lax.dot_general(lhs, pair, dims, preferred_element_type=jnp.float32)
-        tail = lax.dot_general(w1.astype(jnp.bfloat16), s3.astype(jnp.bfloat16), dims, preferred_element_type=jnp.float32)
-        result = main[:count] + (main[count : 2 * count] + (main[2 * count :] + tail))
-        flat = out_ref.reshape(count * nz, LANES)
-        for z in range(nz):
-            flat[pl.ds(z, count, stride=nz), :] = result[:, z * LANES : (z + 1) * LANES]
+        flat = out_ref.reshape(count * group * nz, LANES)
+        for x in range(group):
+            block = jnp.concatenate([columns(ref, x * nz, nz) for ref in part_refs], 0)
+            s1, s2, s3 = three_parts(block)
+            pair = jnp.concatenate([s1, s2], 0).astype(jnp.bfloat16)
+            main = lax.dot_general(lhs, pair, dims, preferred_element_type=jnp.float32)
+            tail = lax.dot_general(
+                w1.astype(jnp.bfloat16), s3.astype(jnp.bfloat16), dims, preferred_element_type=jnp.float32
+            )
+            result = main[:count] + (main[count : 2 * count] + (main[2 * count :] + tail))
+            for z in range(nz):
+                flat[pl.ds(x * nz + z, count, stride=group * nz), :] = result[:, z * LANES : (z + 1) * LANES]
 
     return pl.pallas_call(
         kernel,
-        grid=(nx, halves),
+        grid=(halves, nx // group),
         in_specs=[
-            pl.BlockSpec((count, count), lambda i, h: (0, 0)),
-            *[window(part, nz, lambda i, h: i * halves + h) for part in parts],
+            pl.BlockSpec((count, count), lambda h, i: (0, 0)),
+            *[window(part, group * nz, lambda h, i: h * (nx // group) + i) for part in parts],
         ],
-        out_specs=pl.BlockSpec((count, 1, nz, LANES), lambda i, h: (0, i, 0, h)),
+        out_specs=pl.BlockSpec((count, group, nz, LANES), lambda h, i: (0, i, 0, h)),
         out_shape=jax.ShapeDtypeStruct((count, nx, nz, ny), jnp.float32),
         name="apply_split",
     )(weight, *parts)
@@ -455,10 +487,11 @@
         low_z = shifted(last_z, "gz", True)
         high_z = shifted(first_z, "gz", False)
         halos.append((low_x, high_x, low_z, high_z))
-    parts = [flatten_modes(scaled_modes)]
+    modes, own = flatten_modes(scaled_modes)
+    parts = [modes]
     for (begin, _), halo in zip(SPANS, halos):
         parts.append(criterion(velocity, *halo, begin))
-    mine, other = all_sum(*gram_halves(parts, core))
+    mine, other = all_sum(*gram_halves(parts, own, core))
     weight, triangle, lower_one = factor(mine, other, core, float(total_cells))
     basis = apply_split(weight, parts, cells_x, cells_z, cells_y)
     return basis, triangle, lower_one

time: 106 us -> 104 us (0.981)
  Pallas kernels: 43.5 us -> 42.4 us
  transfers between devices with their start and end apart: 17 -> 17, of which waited for: 10 -> 10; matrix products, arithmetic and copies ran while one was open for 0% -> 0% of each run, Pallas kernels for 11% -> 12%
where the time goes in v2:
time: 104 us; the launch traced here: 103 us
  Pallas kernels  42.4 us (41%)
  starting transfers between devices  29.3 us (28%)
  waiting for transfers between devices  28.8 us (28%)
  local copies, waits for them, and re-layouts  1.74 us (2%)
    ppermute x9, waiting for transfers between devices, flipped(): return lax.ppermute(value, ('gx', 'gz'), pairs)  24.5 us
    ppermute x9, starting transfers between devices, flipped(): return lax.ppermute(value, ('gx', 'gz'), pairs)  16.4 us
    ppermute x8, starting transfers between devices, shifted(): lax.ppermute(value, axis, [(i, (i + step) % count) for i in range(count)])  12.9 us
    pallas_call x2, Pallas kernels, criterion(): pl.pallas_call(kernel, grid=(snaps // group,), in_specs=[pl.BlockSpec((gr...  11.2 us
    pallas_call x1, Pallas kernels, factor(): pl.pallas_call(kernel, in_specs=[pl.BlockSpec(memory_space=pltpu.SMEM), v...  9.46 us
    pallas_call x1, Pallas kernels, apply_split(): pl.pallas_call(kernel, grid=(halves, nx // group), in_specs=[pl.BlockSpec...  6.59 us
    pallas_call x2, Pallas kernels, pack_faces(): pl.pallas_call(kernel, grid=(snaps // group,), in_specs=[pl.BlockSpec(blo...  6.11 us
    pallas_call x1, Pallas kernels, gram_halves(): pl.pallas_call(kernel, grid=(steps,), in_specs=[pl.BlockSpec(memory_space...  4.67 us
  transfers between devices with their start and end apart: 17, of which 10 were waited for; matrix products, arithmetic and copies ran while one was open for 0% of the time, Pallas kernels for 12%

profile of v2, /device:TPU:1, one launch (start us, length us, event | category | flops | bytes accessed | tf_op | source)
XLA Modules:
  0.0 103.2 jit_solution(3629333697116862183)
XLA Ops:
  0.6 3.0 %pack_faces.2 = (f32[32,3,8,256]{3,2,1,0:T(8,128)}, f32[32,3,8,256]{3,2,1,0:T(8,128)}, f32[2,384,128]{2,1,0:T(8,128)}, f32[2,384,128]{2,1,0:T(8,128)}) custom-call(f32[64,3,4,8,256]{4,3,2,1,0:T(8,128)} %v_ref.3, f32[64,3,4,8,256]{4,3,2,1,0:T(8,128)} %v_ref.3), custom_call_target="tpu_custom_call" | custom-call | tf_op jit(solution)/shard_map/pack_faces/pallas_call | solution.py:37
  3.6 2.6 %collective-permute-start = (f32[32,3,8,256]{3,2,1,0:T(8,128)}, f32[32,3,8,256]{3,2,1,0:T(8,128)S(1)}, u32[]{:S(2)}, u32[]{:S(2)}) collective-permute-start(f32[32,3,8,256]{3,2,1,0:T(8,128)} %get-tuple-element.19), channel_id=1, source_target_pairs={{0,8},{8,16},{16,24},{24,32},{32,40},{40,48},{48,56},{56,64},{64,7... | collective-permute-start | bytes 2359304 | tf_op jit(solution)/shard_map/ppermute | solution.py:454
  6.2 1.6 %collective-permute-start.2 = (f32[2,384,128]{2,1,0:T(8,128)}, f32[2,384,128]{2,1,0:T(8,128)S(1)}, u32[]{:S(2)}, u32[]{:S(2)}) collective-permute-start(f32[2,384,128]{2,1,0:T(8,128)} %get-tuple-element.21), channel_id=1, source_target_pairs={{0,1},{1,2},{2,3},{3,4},{4,5},{5,6},{6,7},{7,0},{8,9},{9,10},{10,1... | collective-permute-start | bytes 1179656 | tf_op jit(solution)/shard_map/ppermute | solution.py:454
  7.9 3.9 %collective-permute-start.3 = (f32[2,384,128]{2,1,0:T(8,128)}, f32[2,384,128]{2,1,0:T(8,128)S(1)}, u32[]{:S(2)}, u32[]{:S(2)}) collective-permute-start(f32[2,384,128]{2,1,0:T(8,128)} %get-tuple-element.22), channel_id=1, source_target_pairs={{0,7},{1,0},{2,1},{3,2},{4,3},{5,4},{6,5},{7,6},{8,15},{9,8},{10,9... | collective-permute-start | bytes 1179656 | tf_op jit(solution)/shard_map/ppermute | solution.py:454
  11.8 3.1 %pack_faces.3 = (f32[32,3,8,256]{3,2,1,0:T(8,128)}, f32[32,3,8,256]{3,2,1,0:T(8,128)}, f32[2,384,128]{2,1,0:T(8,128)}, f32[2,384,128]{2,1,0:T(8,128)}) custom-call(f32[64,3,4,8,256]{4,3,2,1,0:T(8,128)} %v_ref.3, f32[64,3,4,8,256]{4,3,2,1,0:T(8,128)} %v_ref.3), custom_call_target="tpu_custom_call" | custom-call | tf_op jit(solution)/shard_map/pack_faces/pallas_call | solution.py:37
  14.9 1.7 %collective-permute-start.4 = (f32[32,3,8,256]{3,2,1,0:T(8,128)}, f32[32,3,8,256]{3,2,1,0:T(8,128)S(1)}, u32[]{:S(2)}, u32[]{:S(2)}) collective-permute-start(f32[32,3,8,256]{3,2,1,0:T(8,128)} %get-tuple-element.23), channel_id=1, source_target_pairs={{0,8},{8,16},{16,24},{24,32},{32,40},{40,48},{48,56},{56,64},{64,7... | collective-permute-start | bytes 2359304 | tf_op jit(solution)/shard_map/ppermute | solution.py:454
  16.6 4.2 %collective-permute-done.2.lz_ref = f32[2,384,128]{2,1,0:T(8,128)S(1)} collective-permute-done((f32[2,384,128]{2,1,0:T(8,128)}, f32[2,384,128]{2,1,0:T(8,128)S(1)}, u32[]{:S(2)}, u32[]{:S(2)}) %collective-permute-start.2) | collective-permute-done | bytes 393248 | tf_op jit(solution)/shard_map/ppermute | solution.py:454
  20.9 0.7 copy-done
  21.6 3.0 %collective-permute-start.7 = (f32[2,384,128]{2,1,0:T(8,128)}, f32[2,384,128]{2,1,0:T(8,128)}, u32[]{:S(2)}, u32[]{:S(2)}) collective-permute-start(f32[2,384,128]{2,1,0:T(8,128)} %get-tuple-element.26), channel_id=1, source_target_pairs={{0,7},{1,0},{2,1},{3,2},{4,3},{5,4},{6,5},{7,6},{8,15},{9,8},{10,9... | collective-permute-start | bytes 1179656 | tf_op jit(solution)/shard_map/ppermute | solution.py:454
  24.6 4.3 %flatten_modes.1 = (f32[64,8192]{1,0:T(8,128)}, f32[3,64,128]{2,1,0:T(8,128)}) custom-call(f32[64,4,8,256]{3,2,1,0:T(8,128)} %m_ref.1), custom_call_target="tpu_custom_call" | custom-call | tf_op jit(solution)/shard_map/flatten_modes/pallas_call | solution.py:74
  28.9 1.0 copy-done.1
  29.9 5.5 %criterion.2.refs_1_ = f32[4,64,8,128]{3,2,1,0:T(8,128)} custom-call(f32[64,3,4,8,256]{4,3,2,1,0:T(8,128)} %v_ref.3, f32[32,3,8,256]{3,2,1,0:T(8,128)S(1)} %collective-permute-done.lx_ref, f32[32,3,8,256]{3,2,1,0:T(8,128)S(1)} %collective-permute-done.1.hx_ref, f32[2,384,128]{2,1,0:T(8,128)S(1)} %collective-permute-done.2.lz_ref, f32[2,384,128]{2,1,0:T(8,128)S(1)} %copy-done.1), custom_call_target="tpu_custom_call" | custom-call | tf_op jit(solution)/shard_map/criterion/pallas_call | solution.py:152
  35.5 5.7 %criterion.3.refs_2_ = f32[4,64,8,128]{3,2,1,0:T(8,128)} custom-call(f32[64,3,4,8,256]{4,3,2,1,0:T(8,128)} %v_ref.3, f32[32,3,8,256]{3,2,1,0:T(8,128)S(1)} %collective-permute-done.4.lx_ref, f32[32,3,8,256]{3,2,1,0:T(8,128)S(1)} %collective-permute-done.5.hx_ref, f32[2,384,128]{2,1,0:T(8,128)} %collective-permute-done.6.lz_ref, ...), custom_call_target="tpu_custom_call" | custom-call | tf_op jit(solution)/shard_map/criterion/pallas_call | solution.py:152
  41.2 4.7 %gram_halves.1 = (f32[2,40,128]{2,1,0:T(8,128)S(1)}, f32[2,40,128]{2,1,0:T(8,128)S(1)}) custom-call(s32[1]{0:T(128)} %bitcast.core_ref, f32[64,8192]{1,0:T(8,128)} %get-tuple-element.18.refs_0_, f32[4,64,8,128]{3,2,1,0:T(8,128)} %criterion.2.refs_1_, f32[4,64,8,128]{3,2,1,0:T(8,128)} %criterion.3.refs_2_, f32[3,64,128]{2,1,0:T(8,128)} %get-tuple-element.27.refs_3_), custom_call_target="tpu_custom_call" | custom-call | tf_op jit(solution)/shard_map/gram_halves/pallas_call | solution.py:394
  45.9 4.6 %collective-permute-start.8 = (f32[2,40,128]{2,1,0:T(8,128)S(1)}, f32[2,40,128]{2,1,0:T(8,128)S(1)}, u32[]{:S(2)}, u32[]{:S(2)}) collective-permute-start(f32[2,40,128]{2,1,0:T(8,128)S(1)} %get-tuple-element.29), channel_id=1, source_target_pairs={{0,8},{1,9},{2,10},{3,11},{4,12},{5,13},{6,14},{7,15},{8,0},{9,1},... | collective-permute-start | bytes 122888 | tf_op jit(solution)/shard_map/ppermute | solution.py:462
  50.5 0.9 collective-permute-done.8
  51.5 2.8 %collective-permute-done.9 = f32[2,40,128]{2,1,0:T(8,128)S(1)} collective-permute-done((f32[2,40,128]{2,1,0:T(8,128)S(1)}, f32[2,40,128]{2,1,0:T(8,128)S(1)}, u32[]{:S(2)}, u32[]{:S(2)}) %collective-permute-start.9) | collective-permute-done | bytes 40992 | tf_op jit(solution)/shard_map/ppermute | solution.py:462
  54.4 4.0 %collective-permute-done.10 = f32[2,40,128]{2,1,0:T(8,128)S(1)} collective-permute-done((f32[2,40,128]{2,1,0:T(8,128)S(1)}, f32[2,40,128]{2,1,0:T(8,128)S(1)}, u32[]{:S(2)}, u32[]{:S(2)}) %collective-permute-start.10) | collective-permute-done | bytes 40992 | tf_op jit(solution)/shard_map/ppermute | solution.py:462
  58.5 0.1 collective-permute-start.11
  58.6 2.8 %collective-permute-done.11 = f32[2,40,128]{2,1,0:T(8,128)S(1)} collective-permute-done((f32[2,40,128]{2,1,0:T(8,128)S(1)}, f32[2,40,128]{2,1,0:T(8,128)S(1)}, u32[]{:S(2)}, u32[]{:S(2)}) %collective-permute-start.11) | collective-permute-done | bytes 40992 | tf_op jit(solution)/shard_map/ppermute | solution.py:462
  61.5 1.3 %collective-permute-start.12 = (f32[2,40,128]{2,1,0:T(8,128)S(1)}, f32[2,40,128]{2,1,0:T(8,128)S(1)}, u32[]{:S(2)}, u32[]{:S(2)}) collective-permute-start(f32[2,40,128]{2,1,0:T(8,128)S(1)} %pad_maximum_fusion.3), channel_id=1, source_target_pairs={{0,192},{1,193},{2,194},{3,195},{4,196},{5,197},{6,198},{7,199},{8... | collective-permute-start | bytes 122888 | tf_op jit(solution)/shard_map/ppermute | solution.py:462
  62.8 2.9 %collective-permute-done.12 = f32[2,40,128]{2,1,0:T(8,128)S(1)} collective-permute-done((f32[2,40,128]{2,1,0:T(8,128)S(1)}, f32[2,40,128]{2,1,0:T(8,128)S(1)}, u32[]{:S(2)}, u32[]{:S(2)}) %collective-permute-start.12) | collective-permute-done | bytes 40992 | tf_op jit(solution)/shard_map/ppermute | solution.py:462
  65.7 0.3 collective-permute-start.13
  65.9 2.8 %collective-permute-done.13 = f32[2,40,128]{2,1,0:T(8,128)S(1)} collective-permute-done((f32[2,40,128]{2,1,0:T(8,128)S(1)}, f32[2,40,128]{2,1,0:T(8,128)S(1)}, u32[]{:S(2)}, u32[]{:S(2)}) %collective-permute-start.13) | collective-permute-done | bytes 40992 | tf_op jit(solution)/shard_map/ppermute | solution.py:462
  68.8 0.1 collective-permute-start.14
  68.9 3.9 %collective-permute-done.14 = f32[2,40,128]{2,1,0:T(8,128)S(1)} collective-permute-done((f32[2,40,128]{2,1,0:T(8,128)S(1)}, f32[2,40,128]{2,1,0:T(8,128)S(1)}, u32[]{:S(2)}, u32[]{:S(2)}) %collective-permute-start.14) | collective-permute-done | bytes 40992 | tf_op jit(solution)/shard_map/ppermute | solution.py:462
  72.8 1.6 %collective-permute-start.15 = (f32[2,40,128]{2,1,0:T(8,128)S(1)}, f32[2,40,128]{2,1,0:T(8,128)S(1)}, u32[]{:S(2)}, u32[]{:S(2)}) collective-permute-start(f32[2,40,128]{2,1,0:T(8,128)S(1)} %pad_maximum_fusion.6), channel_id=1, source_target_pairs={{0,6},{1,7},{2,4},{3,5},{4,2},{5,3},{6,0},{7,1},{8,14},{9,15},{10,... | collective-permute-start | bytes 122888 | tf_op jit(solution)/shard_map/ppermute | solution.py:462
  74.4 3.5 %collective-permute-done.15 = f32[2,40,128]{2,1,0:T(8,128)S(1)} collective-permute-done((f32[2,40,128]{2,1,0:T(8,128)S(1)}, f32[2,40,128]{2,1,0:T(8,128)S(1)}, u32[]{:S(2)}, u32[]{:S(2)}) %collective-permute-start.15) | collective-permute-done | bytes 40992 | tf_op jit(solution)/shard_map/ppermute | solution.py:462
  77.9 8.3 %collective-permute-start.16 = (f32[2,40,128]{2,1,0:T(8,128)S(1)}, f32[2,40,128]{2,1,0:T(8,128)S(1)}, u32[]{:S(2)}, u32[]{:S(2)}) collective-permute-start(f32[2,40,128]{2,1,0:T(8,128)S(1)} %pad_maximum_fusion.7.mine_ref), channel_id=1, source_target_pairs={{0,8},{1,9},{2,10},{3,11},{4,12},{5,13},{6,14},{7,15},{8,0},{9,1},... | collective-permute-start | bytes 122888 | tf_op jit(solution)/shard_map/ppermute | solution.py:462
  86.2 0.9 collective-permute-done.16.other_ref
  87.1 9.5 %factor.1 = (f32[128,128]{1,0:T(8,128)}, f32[128,128]{1,0:T(8,128)}, f32[128,128]{1,0:T(8,128)}) custom-call(s32[1]{0:T(128)} %bitcast.core_ref, f32[2,40,128]{2,1,0:T(8,128)S(1)} %pad_maximum_fusion.7.mine_ref, f32[2,40,128]{2,1,0:T(8,128)S(1)} %collective-permute-done.16.other_ref), custom_call_target="tpu_custom_call" | custom-call | tf_op jit(solution)/shard_map/factor/pallas_call | solution.py:316
  96.6 6.6 %apply_split.1 = f32[128,4,8,256]{3,2,1,0:T(8,128)} custom-call(f32[128,128]{1,0:T(8,128)} %get-tuple-element.30.w_ref, f32[64,8192]{1,0:T(8,128)} %get-tuple-element.18.refs_0_, f32[4,64,8,128]{3,2,1,0:T(8,128)} %criterion.2.refs_1_, f32[4,64,8,128]{3,2,1,0:T(8,128)} %criterion.3.refs_2_), custom_call_target="tpu_custom_call" | custom-call | tf_op jit(solution)/shard_map/apply_split/pallas_call | solution.py:438
  (30 shorter events, 0.4 us)
Async XLA Ops:
  3.6 18.0 %collective-permute-start = (f32[32,3,8,256]{3,2,1,0:T(8,128)}, f32[32,3,8,256]{3,2,1,0:T(8,128)S(1)}, u32[]{:S(2)}, u32[]{:S(2)}) collective-permute-start(f32[32,3,8,256]{3,2,1,0:T(8,128)} %get-tuple-element.19), channel_id=1, source_target_pairs={{0,8},{8,16},{16,24},{24,32},{32,40},{40,48},{48,56},{56,64},{64,7... | collective-permute-start | bytes 2359304 | tf_op jit(solution)/shard_map/ppermute | solution.py:454
  6.2 14.6 %collective-permute-start.2 = (f32[2,384,128]{2,1,0:T(8,128)}, f32[2,384,128]{2,1,0:T(8,128)S(1)}, u32[]{:S(2)}, u32[]{:S(2)}) collective-permute-start(f32[2,384,128]{2,1,0:T(8,128)} %get-tuple-element.21), channel_id=1, source_target_pairs={{0,1},{1,2},{2,3},{3,4},{4,5},{5,6},{6,7},{7,0},{8,9},{9,10},{10,1... | collective-permute-start | bytes 1179656 | tf_op jit(solution)/shard_map/ppermute | solution.py:454
  7.9 13.0 %collective-permute-start.3 = (f32[2,384,128]{2,1,0:T(8,128)}, f32[2,384,128]{2,1,0:T(8,128)S(1)}, u32[]{:S(2)}, u32[]{:S(2)}) collective-permute-start(f32[2,384,128]{2,1,0:T(8,128)} %get-tuple-element.22), channel_id=1, source_target_pairs={{0,7},{1,0},{2,1},{3,2},{4,3},{5,4},{6,5},{7,6},{8,15},{9,8},{10,9... | collective-permute-start | bytes 1179656 | tf_op jit(solution)/shard_map/ppermute | solution.py:454
  11.8 17.1 %collective-permute-start.1 = (f32[32,3,8,256]{3,2,1,0:T(8,128)}, f32[32,3,8,256]{3,2,1,0:T(8,128)S(1)}, u32[]{:S(2)}, u32[]{:S(2)}) collective-permute-start(f32[32,3,8,256]{3,2,1,0:T(8,128)} %get-tuple-element.20), channel_id=1, source_target_pairs={{0,248},{8,0},{16,8},{24,16},{32,24},{40,32},{48,40},{56,48},{64,5... | collective-permute-start | bytes 2359304 | tf_op jit(solution)/shard_map/ppermute | solution.py:454
  14.9 20.5 %collective-permute-start.4 = (f32[32,3,8,256]{3,2,1,0:T(8,128)}, f32[32,3,8,256]{3,2,1,0:T(8,128)S(1)}, u32[]{:S(2)}, u32[]{:S(2)}) collective-permute-start(f32[32,3,8,256]{3,2,1,0:T(8,128)} %get-tuple-element.23), channel_id=1, source_target_pairs={{0,8},{8,16},{16,24},{24,32},{32,40},{40,48},{48,56},{56,64},{64,7... | collective-permute-start | bytes 2359304 | tf_op jit(solution)/shard_map/ppermute | solution.py:454
  20.9 14.6 %collective-permute-start.5 = (f32[32,3,8,256]{3,2,1,0:T(8,128)}, f32[32,3,8,256]{3,2,1,0:T(8,128)S(1)}, u32[]{:S(2)}, u32[]{:S(2)}) collective-permute-start(f32[32,3,8,256]{3,2,1,0:T(8,128)} %get-tuple-element.24), channel_id=1, source_target_pairs={{0,248},{8,0},{16,8},{24,16},{32,24},{40,32},{48,40},{56,48},{64,5... | collective-permute-start | bytes 2359304 | tf_op jit(solution)/shard_map/ppermute | solution.py:454
  20.9 0.7 copy-start
  21.6 13.8 %collective-permute-start.6 = (f32[2,384,128]{2,1,0:T(8,128)}, f32[2,384,128]{2,1,0:T(8,128)}, u32[]{:S(2)}, u32[]{:S(2)}) collective-permute-start(f32[2,384,128]{2,1,0:T(8,128)} %get-tuple-element.25), channel_id=1, source_target_pairs={{0,1},{1,2},{2,3},{3,4},{4,5},{5,6},{6,7},{7,0},{8,9},{9,10},{10,1... | collective-permute-start | bytes 1179656 | tf_op jit(solution)/shard_map/ppermute | solution.py:454
  21.6 13.8 %collective-permute-start.7 = (f32[2,384,128]{2,1,0:T(8,128)}, f32[2,384,128]{2,1,0:T(8,128)}, u32[]{:S(2)}, u32[]{:S(2)}) collective-permute-start(f32[2,384,128]{2,1,0:T(8,128)} %get-tuple-element.26), channel_id=1, source_target_pairs={{0,7},{1,0},{2,1},{3,2},{4,3},{5,4},{6,5},{7,6},{8,15},{9,8},{10,9... | collective-permute-start | bytes 1179656 | tf_op jit(solution)/shard_map/ppermute | solution.py:454
  28.9 1.0 copy-start.1
  45.9 5.5 %collective-permute-start.8 = (f32[2,40,128]{2,1,0:T(8,128)S(1)}, f32[2,40,128]{2,1,0:T(8,128)S(1)}, u32[]{:S(2)}, u32[]{:S(2)}) collective-permute-start(f32[2,40,128]{2,1,0:T(8,128)S(1)} %get-tuple-element.29), channel_id=1, source_target_pairs={{0,8},{1,9},{2,10},{3,11},{4,12},{5,13},{6,14},{7,15},{8,0},{9,1},... | collective-permute-start | bytes 122888 | tf_op jit(solution)/shard_map/ppermute | solution.py:462
  51.4 2.9 %collective-permute-start.9 = (f32[2,40,128]{2,1,0:T(8,128)S(1)}, f32[2,40,128]{2,1,0:T(8,128)S(1)}, u32[]{:S(2)}, u32[]{:S(2)}) collective-permute-start(f32[2,40,128]{2,1,0:T(8,128)S(1)} %pad_maximum_fusion), channel_id=1, source_target_pairs={{0,16},{1,17},{2,18},{3,19},{4,20},{5,21},{6,22},{7,23},{8,24},{9,... | collective-permute-start | bytes 122888 | tf_op jit(solution)/shard_map/ppermute | solution.py:462
  54.3 4.2 %collective-permute-start.10 = (f32[2,40,128]{2,1,0:T(8,128)S(1)}, f32[2,40,128]{2,1,0:T(8,128)S(1)}, u32[]{:S(2)}, u32[]{:S(2)}) collective-permute-start(f32[2,40,128]{2,1,0:T(8,128)S(1)} %pad_maximum_fusion.1), channel_id=1, source_target_pairs={{0,48},{1,49},{2,50},{3,51},{4,52},{5,53},{6,54},{7,55},{8,56},{9,... | collective-permute-start | bytes 122888 | tf_op jit(solution)/shard_map/ppermute | solution.py:462
  58.5 2.9 %collective-permute-start.11 = (f32[2,40,128]{2,1,0:T(8,128)S(1)}, f32[2,40,128]{2,1,0:T(8,128)S(1)}, u32[]{:S(2)}, u32[]{:S(2)}) collective-permute-start(f32[2,40,128]{2,1,0:T(8,128)S(1)} %pad_maximum_fusion.2), channel_id=1, source_target_pairs={{0,64},{1,65},{2,66},{3,67},{4,68},{5,69},{6,70},{7,71},{8,72},{9,... | collective-permute-start | bytes 122888 | tf_op jit(solution)/shard_map/ppermute | solution.py:462
  61.5 4.2 %collective-permute-start.12 = (f32[2,40,128]{2,1,0:T(8,128)S(1)}, f32[2,40,128]{2,1,0:T(8,128)S(1)}, u32[]{:S(2)}, u32[]{:S(2)}) collective-permute-start(f32[2,40,128]{2,1,0:T(8,128)S(1)} %pad_maximum_fusion.3), channel_id=1, source_target_pairs={{0,192},{1,193},{2,194},{3,195},{4,196},{5,197},{6,198},{7,199},{8... | collective-permute-start | bytes 122888 | tf_op jit(solution)/shard_map/ppermute | solution.py:462
  65.7 3.1 %collective-permute-start.13 = (f32[2,40,128]{2,1,0:T(8,128)S(1)}, f32[2,40,128]{2,1,0:T(8,128)S(1)}, u32[]{:S(2)}, u32[]{:S(2)}) collective-permute-start(f32[2,40,128]{2,1,0:T(8,128)S(1)} %pad_maximum_fusion.4), channel_id=1, source_target_pairs={{0,1},{1,0},{2,3},{3,2},{4,5},{5,4},{6,7},{7,6},{8,9},{9,8},{10,11... | collective-permute-start | bytes 122888 | tf_op jit(solution)/shard_map/ppermute | solution.py:462
  68.8 4.0 %collective-permute-start.14 = (f32[2,40,128]{2,1,0:T(8,128)S(1)}, f32[2,40,128]{2,1,0:T(8,128)S(1)}, u32[]{:S(2)}, u32[]{:S(2)}) collective-permute-start(f32[2,40,128]{2,1,0:T(8,128)S(1)} %pad_maximum_fusion.5), channel_id=1, source_target_pairs={{0,2},{1,3},{2,0},{3,1},{4,6},{5,7},{6,4},{7,5},{8,10},{9,11},{10,... | collective-permute-start | bytes 122888 | tf_op jit(solution)/shard_map/ppermute | solution.py:462
  72.8 5.0 %collective-permute-start.15 = (f32[2,40,128]{2,1,0:T(8,128)S(1)}, f32[2,40,128]{2,1,0:T(8,128)S(1)}, u32[]{:S(2)}, u32[]{:S(2)}) collective-permute-start(f32[2,40,128]{2,1,0:T(8,128)S(1)} %pad_maximum_fusion.6), channel_id=1, source_target_pairs={{0,6},{1,7},{2,4},{3,5},{4,2},{5,3},{6,0},{7,1},{8,14},{9,15},{10,... | collective-permute-start | bytes 122888 | tf_op jit(solution)/shard_map/ppermute | solution.py:462
  77.9 9.2 %collective-permute-start.16 = (f32[2,40,128]{2,1,0:T(8,128)S(1)}, f32[2,40,128]{2,1,0:T(8,128)S(1)}, u32[]{:S(2)}, u32[]{:S(2)}) collective-permute-start(f32[2,40,128]{2,1,0:T(8,128)S(1)} %pad_maximum_fusion.7.mine_ref), channel_id=1, source_target_pairs={{0,8},{1,9},{2,10},{3,11},{4,12},{5,13},{6,14},{7,15},{8,0},{9,1},... | collective-permute-start | bytes 122888 | tf_op jit(solution)/shard_map/ppermute | solution.py:462
